TPU v7x, 32 devices: a whole 2x2x4 slice. The times are simulated.
32 devices in a mesh: tm: 8 (over z, core), lat: 4 (over y, x).
Axes of the slice: x: 2, y: 2, z: 4, core: 2. Of those that a mesh axis runs over, the one named last changes fastest.
Arguments:
- states: float32 [4, 8, 128, 2048], P(None, 'tm', 'lat'), may hold values from -6 to 6
- mass_term: float32 [128, 2048], P('lat'), may hold values from 0.005 to 0.05
- lat_coupling: float32 [128, 2048], P('lat'), may hold values from 0.25 to 2
- lon_coupling: float32 [128, 2048], P('lat'), may hold values from 0.25 to 2
Outputs:
- result: float32 [4, 8, 128, 2048], P(None, 'tm', 'lat')
All inputs are finite; a program needn't handle non-finite values.
Results may differ from a plain program's by a relative error of at most 0.0003.
Values sent between devices are 32-bit elements; how exact they have to be, the bound alone decides.
No kernel may reach another device: no remote copies, remote signals or barrier semaphores. Data moves between devices by JAX's collectives and lax.ppermute only.
A program may use at most 64 MiB of HBM per device.

v0:
```python
import math

import jax
import jax.numpy as jnp
import numpy as np
from jax import lax
from jax.experimental import pallas as pl
from jax.experimental.pallas import tpu as pltpu
from jax.sharding import PartitionSpec as P

SWEEPS = 16
HALO = SWEEPS
LEVELS = 4
CHUNK = 37
PAD = 8
LANES = 128
SUB = 8

mass_low = 0.005
mass_high = 0.05
coupling_high = 2.0
base_shift = 0.002
time_coupling = 0.05
CENTER = (mass_low + mass_high + 8.0 * coupling_high) / 2.0
DELTA = (mass_high + 8.0 * coupling_high - mass_low) / 2.0


def frequencies(times):
    index = np.arange(times)
    return np.where(index <= times // 2, index, index - times // 2).astype(np.float64)


def time_basis(times):
    freq = frequencies(times)
    index = np.arange(times)
    angle = 2.0 * np.pi * freq[:, None] * np.arange(times)[None, :] / times
    edge = ((index == 0) | (index == times // 2))[:, None]
    cosine = np.cos(angle) * np.where(edge, math.sqrt(1.0 / times), math.sqrt(2.0 / times))
    sine = np.sin(angle) * math.sqrt(2.0 / times)
    return np.where((index > times // 2)[:, None], sine, cosine)


def weights(times):
    shift = base_shift + time_coupling * (2.0 - 2.0 * np.cos(2.0 * np.pi * frequencies(times) / times))
    sigma = (shift + CENTER) / DELTA
    second = [np.ones_like(sigma), 2.0 * sigma]
    first = [np.ones_like(sigma), sigma]
    for _ in range(SWEEPS):
        second.append(2.0 * sigma * second[-1] - second[-2])
        first.append(2.0 * sigma * first[-1] - first[-2])
    rows = [2.0 * second[SWEEPS - j] / (DELTA * first[SWEEPS + 1]) for j in range(SWEEPS + 1)]
    return 0.5 * np.stack(rows)


def padded_length(width):
    steps = -(-(width + LEVELS - 1) // CHUNK) * CHUNK
    return -(-(PAD + steps + 1) // SUB) * SUB


def run_sweeps(width, times, b_ref, p_ref, q_ref, e_ref, diag_ref, lon_ref, lat_ref, c_ref):
    lanes = b_ref.shape[1]
    trips = -(-(width + LEVELS - 1) // CHUNK)

    def rows(ref, j):
        return ref[pl.ds(pl.multiple_of(j * times, SUB), times), :]

    def wide(ref, j):
        return jnp.broadcast_to(ref[pl.ds(j, 1), :], (times, lanes))

    kept = [(l, -l - k) for l in range(LEVELS) for k in (1, 0)]
    kept += [(name, -k) for name in ("rhs", "diag", "lat") for k in range(1, LEVELS)]
    kept += [("lon", -k) for k in range(1, LEVELS + 1)]

    def one_pass(index, carry):
        c = [
            c_ref[pl.ds(pl.multiple_of((SWEEPS - 1 - LEVELS * index - l) * times, SUB), times), :]
            for l in range(LEVELS)
        ]

        def trip(number, held):
            start = PAD + number * CHUNK
            held = iter(held)
            u = [dict() for _ in range(LEVELS + 1)]
            rhs, diag, lat, lon = {}, {}, {}, {}
            for table, at in kept:
                (u[table] if isinstance(table, int) else dict(rhs=rhs, diag=diag, lat=lat, lon=lon)[table])[at] = next(held)
            for s in range(CHUNK):
                u[0][s + 1] = rows(p_ref, start + s + 1)
                rhs[s] = rows(b_ref, start + s)
                diag[s] = wide(diag_ref, start + s)
                lat[s] = wide(lat_ref, start + s)
                lon[s] = wide(lon_ref, start + s)
                for l in range(LEVELS):
                    i = s - l
                    v = u[l]
                    older = rows(q_ref, start + s) if l == 0 else u[l - 1][i]
                    near = v[i]
                    south = pltpu.roll(lat[i] * near, 1, 1)
                    north = lat[i] * pltpu.roll(near, lanes - 1, 1)
                    total = (c[l] * rhs[i] - older) + (diag[i] * near + lon[i - 1] * v[i - 1])
                    total = total + (north + south)
                    u[l + 1][i] = total + lon[i] * v[i + 1]
                q_ref[pl.ds(pl.multiple_of((start + s - LEVELS + 2) * times, SUB), times), :] = u[LEVELS - 1][
                    s - LEVELS + 2
                ]
                done = s - LEVELS + 1
                where = pl.ds(pl.multiple_of((start + done) * times, SUB), times)
                p_ref[where, :] = u[LEVELS][done]
                e_ref[where, :] = u[LEVELS][done] - u[LEVELS - 2][done]
            tables = dict(rhs=rhs, diag=diag, lat=lat, lon=lon)
            return tuple((u[table] if isinstance(table, int) else tables[table])[CHUNK + at] for table, at in kept)

        zero = jnp.zeros((times, lanes), jnp.float32)
        lax.fori_loop(0, trips, trip, tuple(rows(p_ref, PAD) if at == (0, 0) else zero for at in kept))
        return carry

    lax.fori_loop(0, SWEEPS // LEVELS, one_pass, 0)


R2 = math.sqrt(0.5)


def spread(x):
    e1, e2, e3 = x[1] + x[7], x[2] + x[6], x[3] + x[5]
    o1, o2, o3 = x[1] - x[7], x[2] - x[6], x[3] - x[5]
    a, b = x[0] + x[4], x[0] - x[4]
    p, m, q, n = e1 + e3, R2 * (e1 - e3), a + e2, R2 * (o1 + o3)
    return [q + p, b + m, a - e2, b - m, q - p, n + o2, o1 - o3, n - o2]


def gather_times(v):
    s, d = v[0] + v[4], v[0] - v[4]
    m, p, n = R2 * (v[1] - v[3]), v[1] + v[3], R2 * (v[5] + v[7])
    sv, g, h = s + v[2], s - v[2], v[5] - v[7]
    dp, dm, np_, nm = d + m, d - m, n + v[6], n - v[6]
    return [sv + p, dp + np_, g + h, dm + nm, sv - p, dm - nm, g - h, dp - np_]


def halo_group(pieces, width):
    lane = lax.broadcasted_iota(jnp.int32, (SUB, LANES), 1)
    groups = LANES // width
    out = []
    for q in range(groups):
        tile = None
        for g, piece in enumerate(pieces):
            moved = piece if g == q else pltpu.roll(piece, (width * (g - q)) % LANES, 1)
            tile = moved if tile is None else jnp.where(lane < width * g, tile, moved)
        out.append(tile)
    return out


def pack_kernel(width, band_ref, s_ref, m_ref, y_ref, x_ref, send_ref, coef_ref):
    bands = s_ref.shape[2] // width
    rl = s_ref.shape[1]
    lane = lax.broadcasted_iota(jnp.int32, (rl, LANES), 1)
    small = lax.broadcasted_iota(jnp.int32, (SUB, LANES), 1)
    group = 2 * HALO

    def pack(west, east):
        both = pltpu.roll(jnp.where(lane < LANES // 2, east, west), HALO, 1)
        tile = None
        for q in range(rl // SUB):
            piece = both[q * SUB : (q + 1) * SUB]
            moved = piece if q == 0 else pltpu.roll(piece, group * q, 1)
            tile = moved if tile is None else jnp.where(small < group * q, tile, moved)
        return tile

    tiles = width // LANES
    total = bands * width
    for f in range(s_ref.shape[0]):
        for i in range(bands):
            for h in range(tiles):
                lo = i * width + h * LANES
                send_ref[i, f, h * rl : (h + 1) * rl, :] = s_ref[f, :, lo : lo + LANES]
            lo_w = (i * width - LANES) % total
            lo_e = ((i + 1) * width) % total
            send_ref[i, f, tiles * rl :, :] = pack(s_ref[f, :, lo_w : lo_w + LANES], s_ref[f, :, lo_e : lo_e + LANES])
    band = band_ref[0]
    lo = pl.multiple_of(band * width, LANES)
    lo_w = pl.multiple_of(lax.rem(band * width + (total - LANES), total), LANES)
    lo_e = pl.multiple_of(lax.rem((band + 1) * width, total), LANES)
    for n, ref in enumerate((m_ref, y_ref, x_ref)):
        for h in range(tiles):
            coef_ref[n, h * rl : (h + 1) * rl, :] = ref[:, pl.ds(lo + h * LANES, LANES)]
        coef_ref[n, tiles * rl :, :] = pack(ref[:, pl.ds(lo_w, LANES)], ref[:, pl.ds(lo_e, LANES)])


def finish_coefficients(m, y, x):
    scale = 2.0 / DELTA
    lane = lax.broadcasted_iota(jnp.int32, m.shape, 1)
    south = jnp.where(lane == 0, 0.0, pltpu.roll(y, 1, 1))
    west = pltpu.roll(x, 1, 0)
    diag = scale * (CENTER - m - (y + south) - (x + west))
    return diag, scale * x, jnp.where(lane == m.shape[1] - 1, 0.0, scale * y)


def coef_kernel(width, g_ref, diag_ref, lon_ref, lat_ref, t_ref, tile_ref):
    lats, count, _, _ = g_ref.shape
    tiles = width // LANES
    rl = (g_ref.shape[2] * LANES - 0) // (width + 2 * HALO)
    for n in range(count):
        for h in range(tiles):
            for l in range(lats):
                tile_ref[l * rl : (l + 1) * rl, :] = g_ref[l, n, h * rl : (h + 1) * rl, :]
            t_ref[n, HALO + h * LANES : HALO + (h + 1) * LANES, :] = tile_ref[...].T
    for l in range(lats):
        got = halo_group([g_ref[l, n, tiles * rl :, :] for n in range(count)], 2 * HALO)
        for q, piece in enumerate(got):
            tile_ref[l * rl + q * SUB : l * rl + (q + 1) * SUB, :] = piece
    turned = tile_ref[...].T
    for n in range(count):
        t_ref[n, :HALO, :] = turned[n * 2 * HALO : n * 2 * HALO + HALO]
        t_ref[n, HALO + width :, :] = turned[n * 2 * HALO + HALO : (n + 1) * 2 * HALO]
    out = finish_coefficients(t_ref[0], t_ref[1], t_ref[2])
    full = width + 2 * HALO
    for ref, value in zip((diag_ref, lon_ref, lat_ref), out):
        ref[:PAD, :] = jnp.zeros((PAD, ref.shape[1]), jnp.float32)
        ref[PAD : PAD + full, :] = value
        ref[PAD + full :, :] = jnp.zeros((ref.shape[0] - PAD - full, ref.shape[1]), jnp.float32)


def solve_kernel(width, first, g_ref, diag_ref, lon_ref, lat_ref, c_ref, out_ref, b_ref, p_ref, q_ref, e_ref, t_ref, tile_ref):
    full = width + 2 * HALO
    times = t_ref.shape[0]
    lats = g_ref.shape[0] // times
    tiles = width // LANES
    rl = t_ref.shape[2] // lats
    for t in range(times):
        for h in range(tiles):
            turned = jnp.concatenate([g_ref[t * lats + l, h * rl : (h + 1) * rl, :] for l in range(lats)], 0).T
            t_ref[t, HALO + h * LANES : HALO + (h + 1) * LANES, :] = turned
    per = LANES // (2 * HALO)
    for g in range(times // per):
        for l in range(lats):
            got = halo_group([g_ref[(g * per + n) * lats + l, tiles * rl :, :] for n in range(per)], 2 * HALO)
            for q, piece in enumerate(got):
                tile_ref[l * rl + q * SUB : l * rl + (q + 1) * SUB, :] = piece
        turned = tile_ref[...].T
        for n in range(per):
            t_ref[g * per + n, :HALO, :] = turned[n * 2 * HALO : n * 2 * HALO + HALO]
            t_ref[g * per + n, HALO + width :, :] = turned[n * 2 * HALO + HALO : (n + 1) * 2 * HALO]

    lanes = b_ref.shape[1]
    head = PAD * times
    tail = (PAD + full) * times
    for ref in (b_ref, p_ref):
        ref[:head, :] = jnp.zeros((head, lanes), jnp.float32)
        ref[tail:, :] = jnp.zeros((ref.shape[0] - tail, lanes), jnp.float32)
    q_ref[...] = jnp.zeros(q_ref.shape, jnp.float32)

    def to_frequencies(block, carry):
        lo = pl.multiple_of(block * SUB, SUB)
        v = spread([t_ref[t, pl.ds(lo, SUB), :] for t in range(times)])
        for k in range(times):
            where = pl.ds((PAD + lo) * times + k, SUB, stride=times)
            b_ref[where, :] = v[k]
            p_ref[where, :] = v[k] * float(first[k])
        return carry

    lax.fori_loop(0, full // SUB, to_frequencies, 0)
    run_sweeps(full, times, b_ref, p_ref, q_ref, e_ref, diag_ref, lon_ref, lat_ref, c_ref)

    def to_times(block, carry):
        lo = pl.multiple_of(block * SUB, SUB)
        base = (PAD + HALO + lo) * times
        v = gather_times([e_ref[pl.ds(base + k, SUB, stride=times), :] for k in range(times)])
        for t in range(times):
            t_ref[t, pl.ds(lo, SUB), :] = v[t]
        return carry

    lax.fori_loop(0, width // SUB, to_times, 0)
    for t in range(times):
        for h in range(tiles):
            turned = t_ref[t, h * LANES : (h + 1) * LANES, :].T
            for l in range(lats):
                out_ref[t * lats + l, h * rl : (h + 1) * rl, :] = turned[l * rl : (l + 1) * rl]


def sweep_kernel(width, b_in, diag_ref, lon_ref, lat_ref, c_ref, e_ref, p_ref, q_ref):
    times = c_ref.shape[0] // (SWEEPS + 1)
    top = c_ref[SWEEPS * times :, :]

    def begin(j, carry):
        where = pl.ds(pl.multiple_of(j * times, SUB), times)
        p_ref[where, :] = top * b_in[where, :]
        return carry

    lax.fori_loop(0, b_in.shape[0] // times, begin, 0)
    q_ref[...] = jnp.zeros(q_ref.shape, jnp.float32)
    run_sweeps(width, times, b_in, p_ref, q_ref, e_ref, diag_ref, lon_ref, lat_ref, c_ref)


VMEM = pl.BlockSpec(memory_space=pltpu.VMEM)
SMEM = pl.BlockSpec(memory_space=pltpu.SMEM)


def params(limit=None):
    return pltpu.CompilerParams(vmem_limit_bytes=limit)


def gather_rows(block, axis):
    count = lax.axis_size(axis)
    me = lax.axis_index(axis)
    got = block[None]
    step = 1
    while step < count:
        other = lax.ppermute(got, axis, [(i, i ^ step) for i in range(count)])
        low = (me & step) == 0
        got = jnp.concatenate([jnp.where(low, got, other), jnp.where(low, other, got)], 0)
        step *= 2
    return got


def solve_packed(states, mass_term, lat_coupling, lon_coupling):
    fields, _, rl, nlon = states.shape
    times, lats = lax.axis_size("tm"), lax.axis_size("lat")
    width = nlon // times
    rows = rl * lats
    full = width + 2 * HALO
    height = full * rl // LANES
    length = padded_length(full)
    f32 = jnp.float32
    band = lax.axis_index("tm").astype(jnp.int32).reshape(1)
    send, coef = pl.pallas_call(
        lambda *refs: pack_kernel(width, *refs),
        out_shape=(
            jax.ShapeDtypeStruct((times, lats, height, LANES), f32),
            jax.ShapeDtypeStruct((3, height, LANES), f32),
        ),
        in_specs=[SMEM] + [VMEM] * 4,
        out_specs=(VMEM, VMEM),
        cost_estimate=pl.CostEstimate(flops=0, transcendentals=0, bytes_accessed=8 * states.size),
        name="pack",
    )(band, states.reshape(fields, rl, nlon), mass_term, lat_coupling, lon_coupling)
    coefs = gather_rows(coef, "lat")
    got = lax.all_to_all(send.reshape(times * lats, height, LANES), ("tm", "lat"), 0, 0, tiled=True)
    line = jax.ShapeDtypeStruct((length, rows), f32)
    diag, lon, lat = pl.pallas_call(
        lambda *refs: coef_kernel(width, *refs),
        out_shape=(line,) * 3,
        in_specs=[VMEM],
        out_specs=(VMEM,) * 3,
        scratch_shapes=[pltpu.VMEM((3, full, rows), f32), pltpu.VMEM((rows, LANES), f32)],
        cost_estimate=pl.CostEstimate(flops=30 * full * rows, transcendentals=0, bytes_accessed=24 * full * rows),
        name="coefficients",
    )(coefs)
    basis = time_basis(times)
    scale = np.max(np.abs(basis), 1) ** 2
    scale = np.where(scale > 1.5 / times, 2.0 / times, 1.0 / times)
    c = weights(times) * scale[None, :]
    c_rows = jnp.broadcast_to(jnp.asarray(c.reshape(-1, 1), f32), ((SWEEPS + 1) * times, rows))
    slab = pltpu.VMEM((length * times, rows), f32)
    out = pl.pallas_call(
        lambda *refs: solve_kernel(width, c[SWEEPS], *refs),
        out_shape=jax.ShapeDtypeStruct((times * lats, width * rl // LANES, LANES), f32),
        in_specs=[VMEM] * 5,
        out_specs=VMEM,
        scratch_shapes=[slab] * 4 + [pltpu.VMEM((times, full, rows), f32), pltpu.VMEM((rows, LANES), f32)],
        cost_estimate=pl.CostEstimate(
            flops=12 * SWEEPS * full * times * rows, transcendentals=0, bytes_accessed=8 * full * times * rows
        ),
        name="solve",
    )(got, diag, lon, lat, c_rows)
    back = lax.all_to_all(out, ("tm", "lat"), 0, 0, tiled=True)
    back = back.reshape(times, lats, width // LANES, rl, LANES)
    return back.transpose(1, 3, 0, 2, 4).reshape(fields, 1, rl, nlon)


def solve_general(states, mass_term, lat_coupling, lon_coupling):
    fields, tl, rl, nlon = states.shape
    tm, lats = lax.axis_size("tm"), lax.axis_size("lat")
    times, rows, parts = tl * tm, rl * lats, lats // fields
    width = nlon // (tm * parts)
    full = width + 2 * HALO
    length = padded_length(full)
    f32 = jnp.float32

    def wrapped(a):
        return jnp.concatenate([a[..., nlon - HALO :], a, a[..., :HALO]], -1)

    wide = wrapped(states)
    bands = jnp.stack([wide[..., n * width : n * width + full] for n in range(tm * parts)])
    bands = bands.reshape(tm, parts, fields, tl, rl, full).transpose(0, 2, 1, 3, 4, 5)
    got = lax.all_to_all(bands.reshape(tm * lats, tl, rl, full), ("tm", "lat"), 0, 0, tiled=True)
    field = got.reshape(tm, lats, tl, rl, full).transpose(4, 0, 2, 1, 3).reshape(full, times, rows)
    basis = jnp.asarray(time_basis(times), f32)
    b = jnp.einsum("kt,jtr->jkr", basis, field, precision=lax.Precision.HIGHEST)
    coef = wrapped(jnp.stack([mass_term, lat_coupling, lon_coupling]))
    first = lax.axis_index("tm") * parts
    mine = jnp.stack([lax.dynamic_slice_in_dim(coef, (first + n) * width, full, 2) for n in range(parts)])
    mine = jnp.broadcast_to(mine[None], (fields,) + mine.shape).reshape(lats, 3, rl, full)
    all_rows = lax.all_to_all(mine, "lat", 0, 0, tiled=True)
    m, y, x = all_rows.transpose(1, 3, 0, 2).reshape(3, full, rows)
    scale = 2.0 / DELTA
    south = jnp.concatenate([jnp.zeros((full, 1), f32), y[:, :-1]], 1)
    diag = scale * (CENTER - m - (y + south) - (x + jnp.roll(x, 1, 0)))
    lat = scale * jnp.concatenate([y[:, :-1], jnp.zeros((full, 1), f32)], 1)
    ends = ((PAD, length - PAD - full), (0, 0))
    diag, lon, lat = (jnp.pad(a, ends) for a in (diag, scale * x, lat))
    b = jnp.pad(b, (ends[0], (0, 0), (0, 0))).reshape(length * times, rows)
    c = weights(times)
    c_rows = jnp.broadcast_to(jnp.asarray(c.reshape(-1, 1), f32), ((SWEEPS + 1) * times, rows))
    slab = pltpu.VMEM((length * times, rows), f32)
    solved = pl.pallas_call(
        lambda *refs: sweep_kernel(full, *refs),
        out_shape=jax.ShapeDtypeStruct((length * times, rows), f32),
        in_specs=[VMEM] * 5,
        out_specs=VMEM,
        scratch_shapes=[slab] * 2,
        name="sweeps",
    )(b, diag, lon, lat, c_rows)
    solved = solved.reshape(length, times, rows)[PAD + HALO : PAD + HALO + width]
    field = jnp.einsum("kt,jkr->jtr", basis, solved, precision=lax.Precision.HIGHEST)
    field = field.reshape(width, tm, tl, lats, rl).transpose(1, 3, 2, 4, 0).reshape(tm * lats, tl, rl, width)
    back = lax.all_to_all(field, ("tm", "lat"), 0, 0, tiled=True)
    back = back.reshape(tm, fields, parts, tl, rl, width).transpose(1, 3, 4, 0, 2, 5)
    return back.reshape(fields, tl, rl, nlon)


def per_device(states, mass_term, lat_coupling, lon_coupling):
    fields, tl, rl, nlon = states.shape
    tm, lats = lax.axis_size("tm"), lax.axis_size("lat")
    packed = tl == 1 and tm == SUB and lats == fields and rl * lats == LANES
    packed = packed and nlon % (tm * LANES) == 0 and 2 * HALO * rl == SUB * LANES
    plan = solve_packed if packed else solve_general
    return plan(states, mass_term, lat_coupling, lon_coupling)


def solution(mesh):
    placed = (P(None, "tm", "lat", None), P("lat", None), P("lat", None), P("lat", None))
    return jax.shard_map(
        per_device,
        mesh=mesh,
        in_specs=placed,
        out_specs=P(None, "tm", "lat", None),
        check_vma=False,
    )
```

profile of v0, /device:TPU:0, one launch (start us, length us, event | category | flops | bytes accessed | tf_op | source)
XLA Modules:
  0.0 97.7 jit_solution(2155501605821515944)
XLA Ops:
  0.0 3.8 %pack.1 = (f32[8,4,72,128]{3,2,1,0:T(8,128)}, f32[3,72,128]{2,1,0:T(8,128)}) custom-call(s32[1]{0:T(128)} %bitcast.refs_0_, f32[4,32,2048]{2,1,0:T(8,128)} %bitcast.11, f32[32,2048]{1,0:T(8,128)} %refs_2_.1, f32[32,2048]{1,0:T(8,128)} %refs_3_.1, f32[32,2048]{1,0:T(8,128)} %refs_4_.1), custom_call_target="tpu_custom_call" | custom-call | bytes 2097152 | tf_op jit(solution)/shard_map/pack/pallas_call | solution.py:324
  3.8 0.0 copy-start.1
  3.8 7.3 %all-to-all-start = ((f32[32,72,128]{2,1,0:T(8,128)}), f32[32,72,128]{2,1,0:T(8,128)S(1)}, u32[]{:S(2)}, u32[]{:S(2)}) async-start(f32[32,72,128]{2,1,0:T(8,128)} %bitcast.10), calls=%async_computation | async-start | bytes 2359296 | tf_op jit(solution)/shard_map/all_to_all | solution.py:336
  11.2 0.0 copy-done.1
  11.2 1.8 %collective-permute-start = (f32[1,3,72,128]{3,2,1,0:T(8,128)S(1)}, f32[1,3,72,128]{3,2,1,0:T(8,128)S(1)}, u32[]{:S(2)}, u32[]{:S(2)}) collective-permute-start(f32[1,3,72,128]{3,2,1,0:T(8,128)S(1)} %bitcast.12), channel_id=1, source_target_pairs={{0,1},{1,0},{2,3},{3,2},{4,5},{5,4},{6,7},{7,6},{8,9},{9,8},{10,11... | collective-permute-start | bytes 331784 | tf_op jit(solution)/shard_map/ppermute | solution.py:307
  13.0 12.0 %collective-permute-done = f32[1,3,72,128]{3,2,1,0:T(8,128)S(1)} collective-permute-done((f32[1,3,72,128]{3,2,1,0:T(8,128)S(1)}, f32[1,3,72,128]{3,2,1,0:T(8,128)S(1)}, u32[]{:S(2)}, u32[]{:S(2)}) %collective-permute-start) | collective-permute-done | bytes 110624 | tf_op jit(solution)/shard_map/ppermute | solution.py:307
  25.0 0.0 copy-start.2
  25.1 0.5 collective-permute-start.1
  25.6 8.2 %collective-permute-done.1 = f32[2,3,72,128]{3,2,1,0:T(8,128)S(1)} collective-permute-done((f32[2,3,72,128]{3,2,1,0:T(8,128)S(1)}, f32[2,3,72,128]{3,2,1,0:T(8,128)S(1)}, u32[]{:S(2)}, u32[]{:S(2)}) %collective-permute-start.1) | collective-permute-done | bytes 221216 | tf_op jit(solution)/shard_map/ppermute | solution.py:307
  33.8 0.8 pad_maximum_fusion.refs_0_
  34.6 2.2 %coefficients.1 = (f32[312,128]{1,0:T(8,128)}, f32[312,128]{1,0:T(8,128)}, f32[312,128]{1,0:T(8,128)}) custom-call(f32[4,3,72,128]{3,2,1,0:T(8,128)} %pad_maximum_fusion.refs_0_), custom_call_target="tpu_custom_call" | custom-call | flops 1105920 | bytes 884736 | tf_op jit(solution)/shard_map/coefficients/pallas_call | solution.py:338
  36.8 3.5 %all-to-all-done.refs_0_ = f32[32,72,128]{2,1,0:T(8,128)S(1)} async-done(((f32[32,72,128]{2,1,0:T(8,128)}), f32[32,72,128]{2,1,0:T(8,128)S(1)}, u32[]{:S(2)}, u32[]{:S(2)}) %all-to-all-start) | async-done | bytes 1179680 | tf_op jit(solution)/shard_map/all_to_all | solution.py:336
  40.3 0.0 copy-start
  40.3 0.0 copy-done.2
  40.3 0.8 broadcast_in_dim.12.refs_4_
  41.1 0.2 copy-done
  41.3 23.7 %solve.1 = f32[32,64,128]{2,1,0:T(8,128)} custom-call(f32[32,72,128]{2,1,0:T(8,128)} %copy-done, f32[312,128]{1,0:T(8,128)} %get-tuple-element.12.refs_1_, f32[312,128]{1,0:T(8,128)} %get-tuple-element.13.refs_2_, f32[312,128]{1,0:T(8,128)} %get-tuple-element.14.refs_3_, f32[136,128]{1,0:T(8,128)} %broadcast_in_dim.12.refs_4_), custom_call_target="tpu_custom_call" | custom-call | flops 56623104 | bytes 2359296 | tf_op jit(solution)/shard_map/solve/pallas_call | solution.py:353
  65.0 30.1 %all_to_all.10 = f32[32,64,128]{2,1,0:T(8,128)S(1)} all-to-all(f32[32,64,128]{2,1,0:T(8,128)} %solve.1), channel_id=1, replica_groups=mesh['tm'=8,'lat'=4] {'tm','lat'}, dimensions={0} | all-to-all | bytes 2097152 | tf_op jit(solution)/shard_map/all_to_all | solution.py:364
  95.0 0.8 copy.6
  95.9 1.8 %reshape.19 = f32[4,1,32,2048]{3,2,1,0:T(8,128)} reshape(f32[4,32,8,2,128]{4,3,2,1,0:T(2,128)S(1)} %copy.6) | data formatting | bytes 2097152 | tf_op jit(solution)/shard_map/reshape | solution.py:366
  (3 shorter events, 0.1 us)
Async XLA Ops:
  3.8 7.3 %copy-start.1 = (f32[3,72,128]{2,1,0:T(8,128)S(1)}, f32[3,72,128]{2,1,0:T(8,128)}, u32[]{:S(2)}) copy-start(f32[3,72,128]{2,1,0:T(8,128)} %get-tuple-element.11) | copy-start | bytes 331780
  3.8 36.4 %all-to-all-start = ((f32[32,72,128]{2,1,0:T(8,128)}), f32[32,72,128]{2,1,0:T(8,128)S(1)}, u32[]{:S(2)}, u32[]{:S(2)}) async-start(f32[32,72,128]{2,1,0:T(8,128)} %bitcast.10), calls=%async_computation | async-start | bytes 2359296 | tf_op jit(solution)/shard_map/all_to_all | solution.py:336
  11.2 13.8 %collective-permute-start = (f32[1,3,72,128]{3,2,1,0:T(8,128)S(1)}, f32[1,3,72,128]{3,2,1,0:T(8,128)S(1)}, u32[]{:S(2)}, u32[]{:S(2)}) collective-permute-start(f32[1,3,72,128]{3,2,1,0:T(8,128)S(1)} %bitcast.12), channel_id=1, source_target_pairs={{0,1},{1,0},{2,3},{3,2},{4,5},{5,4},{6,7},{7,6},{8,9},{9,8},{10,11... | collective-permute-start | bytes 331784 | tf_op jit(solution)/shard_map/ppermute | solution.py:307
  25.0 15.2 %copy-start.2 = (f32[136]{0:T(256)S(1)}, f32[136]{0:T(256)}, u32[]{:S(2)}) copy-start(f32[136]{0:T(256)} %constant.19) | copy-start | bytes 1636
  25.1 8.7 %collective-permute-start.1 = (f32[2,3,72,128]{3,2,1,0:T(8,128)S(1)}, f32[2,3,72,128]{3,2,1,0:T(8,128)S(1)}, u32[]{:S(2)}, u32[]{:S(2)}) collective-permute-start(f32[2,3,72,128]{3,2,1,0:T(8,128)S(1)} %pad_maximum_fusion.1), channel_id=1, source_target_pairs={{0,2},{1,3},{2,0},{3,1},{4,6},{5,7},{6,4},{7,5},{8,10},{9,11},{10,... | collective-permute-start | bytes 663560 | tf_op jit(solution)/shard_map/ppermute | solution.py:307
  40.3 1.1 %copy-start = (f32[32,72,128]{2,1,0:T(8,128)}, f32[32,72,128]{2,1,0:T(8,128)S(1)}, u32[]{:S(2)}) copy-start(f32[32,72,128]{2,1,0:T(8,128)S(1)} %all-to-all-done.refs_0_) | copy-start | bytes 3538948
where the time goes:
time: 98.1 us; the launch traced here: 97.7 us
  blocking collectives  30.1 us (31%)
  Pallas kernels  29.7 us (30%)
  waiting for transfers between devices  23.6 us (24%)
  starting transfers between devices  9.67 us (10%)
  local copies, waits for them, and re-layouts  3.68 us (4%)
    all_to_all x1, blocking collectives, solve_packed(): back = lax.all_to_all(out, ('tm', 'lat'), 0, 0, tiled=True)  30.1 us
    pallas_call x1, Pallas kernels, solve_packed(): pl.pallas_call(lambda *refs: solve_kernel(width, c[SWEEPS], *refs), out_s...  23.7 us
    ppermute x2, waiting for transfers between devices, gather_rows(): other = lax.ppermute(got, axis, [(i, i ^ step) for i in range(count)])  20.2 us
    all_to_all x1, starting transfers between devices, solve_packed(): lax.all_to_all(send.reshape(times * lats, height, LANES), ('tm', 'lat'),...  7.33 us
    pallas_call x1, Pallas kernels, solve_packed(): pl.pallas_call(lambda *refs: pack_kernel(width, *refs), out_shape=(jax.Sh...  3.84 us
    all_to_all x1, waiting for transfers between devices, solve_packed(): lax.all_to_all(send.reshape(times * lats, height, LANES), ('tm', 'lat'),...  3.49 us
    ppermute x2, starting transfers between devices, gather_rows(): other = lax.ppermute(got, axis, [(i, i ^ step) for i in range(count)])  2.35 us
    pallas_call x1, Pallas kernels, solve_packed(): pl.pallas_call(lambda *refs: coef_kernel(width, *refs), out_shape=(line,)...  2.18 us
  transfers between devices with their start and end apart: 3, of which 3 were waited for; matrix products, arithmetic and copies ran while one was open for 1% of the time, Pallas kernels for 2%

commit v1 on v0

v1 whole, which is shorter than its diff:
```python
import math

import jax
import jax.numpy as jnp
import numpy as np
from jax import lax
from jax.experimental import pallas as pl
from jax.experimental.pallas import tpu as pltpu
from jax.sharding import PartitionSpec as P

SWEEPS = 16
HALO = SWEEPS
PACK_BANDS = 2
PAD = 8
LANES = 128
SUB = 8

mass_low = 0.005
mass_high = 0.05
coupling_high = 2.0
base_shift = 0.002
time_coupling = 0.05
CENTER = (mass_low + mass_high + 8.0 * coupling_high) / 2.0
DELTA = (mass_high + 8.0 * coupling_high - mass_low) / 2.0


def frequencies(times):
    index = np.arange(times)
    return np.where(index <= times // 2, index, index - times // 2).astype(np.float64)


def time_basis(times):
    freq = frequencies(times)
    index = np.arange(times)
    angle = 2.0 * np.pi * freq[:, None] * np.arange(times)[None, :] / times
    edge = ((index == 0) | (index == times // 2))[:, None]
    cosine = np.cos(angle) * np.where(edge, math.sqrt(1.0 / times), math.sqrt(2.0 / times))
    sine = np.sin(angle) * math.sqrt(2.0 / times)
    return np.where((index > times // 2)[:, None], sine, cosine)


def weights(times):
    shift = base_shift + time_coupling * (2.0 - 2.0 * np.cos(2.0 * np.pi * frequencies(times) / times))
    sigma = (shift + CENTER) / DELTA
    second = [np.ones_like(sigma), 2.0 * sigma]
    first = [np.ones_like(sigma), sigma]
    for _ in range(SWEEPS):
        second.append(2.0 * sigma * second[-1] - second[-2])
        first.append(2.0 * sigma * first[-1] - first[-2])
    rows = [2.0 * second[SWEEPS - j] / (DELTA * first[SWEEPS + 1]) for j in range(SWEEPS + 1)]
    return 0.5 * np.stack(rows)


def padded_length(width):
    return -(-(PAD + width + 1) // SUB) * SUB


def run_sweeps(columns, rows, b_ref, p_ref, q_ref, diag_ref, lon_ref, lat_ref, c_ref):
    stride = rows + PAD
    turn = SUB

    def sweep(c, new_ref, old_ref, place_ref, last=False, gain=None):
        for block in range(rows // SUB):

            def at(ref, column, shift=0):
                lo = column * stride + PAD + block * SUB + shift
                return ref[lo : lo + SUB, :]

            def coef(ref, column):
                lo = column * rows + block * SUB
                return ref[lo : lo + SUB, :]

            final = columns - 1
            for n in range(columns):
                near = at(new_ref, n)
                east = at(new_ref, n + 1) if n < final else pltpu.roll(at(new_ref, 0), LANES - turn, 1)
                west = at(new_ref, n - 1) if n > 0 else pltpu.roll(at(new_ref, final), turn, 1)
                lon_west = coef(lon_ref, n - 1) if n > 0 else pltpu.roll(coef(lon_ref, final), turn, 1)
                image = (coef(diag_ref, n) * near + coef(lon_ref, n) * east) + lon_west * west
                image = image + at(lat_ref, n) * at(new_ref, n, 1) + at(lat_ref, n, -1) * at(new_ref, n, -1)
                if gain is not None:
                    image = gain * image
                total = c * at(b_ref, n) + image
                if old_ref is not None:
                    total = total - at(old_ref, n)
                if last:
                    total = total - at(old_ref, n)
                lo = n * stride + PAD + block * SUB
                place_ref[lo : lo + SUB, :] = total

    def wide(degree):
        return jnp.broadcast_to(c_ref[pl.ds(degree, 1), :], (SUB, LANES))

    top = wide(SWEEPS)
    sweep(wide(SWEEPS - 1), b_ref, None, q_ref, gain=top)
    sweep(wide(SWEEPS - 2) - top, q_ref, None, p_ref)

    def pair(index, carry):
        sweep(wide(SWEEPS - 3 - 2 * index), p_ref, q_ref, q_ref)
        sweep(wide(SWEEPS - 4 - 2 * index), q_ref, p_ref, p_ref)
        return carry

    lax.fori_loop(0, SWEEPS // 2 - 2, pair, 0)
    sweep(wide(1), p_ref, q_ref, q_ref)
    sweep(wide(0), q_ref, p_ref, p_ref, last=True)


R2 = math.sqrt(0.5)


def spread(x):
    e1, e2, e3 = x[1] + x[7], x[2] + x[6], x[3] + x[5]
    o1, o2, o3 = x[1] - x[7], x[2] - x[6], x[3] - x[5]
    a, b = x[0] + x[4], x[0] - x[4]
    p, m, q, n = e1 + e3, R2 * (e1 - e3), a + e2, R2 * (o1 + o3)
    return [q + p, b + m, a - e2, b - m, q - p, n + o2, o1 - o3, n - o2]


def gather_times(v):
    s, d = v[0] + v[4], v[0] - v[4]
    m, p, n = R2 * (v[1] - v[3]), v[1] + v[3], R2 * (v[5] + v[7])
    sv, g, h = s + v[2], s - v[2], v[5] - v[7]
    dp, dm, np_, nm = d + m, d - m, n + v[6], n - v[6]
    return [sv + p, dp + np_, g + h, dm + nm, sv - p, dm - nm, g - h, dp - np_]


def halo_group(pieces, width):
    lane = lax.broadcasted_iota(jnp.int32, (SUB, LANES), 1)
    groups = LANES // width
    out = []
    for q in range(groups):
        tile = None
        for g, piece in enumerate(pieces):
            moved = piece if g == q else pltpu.roll(piece, (width * (g - q)) % LANES, 1)
            tile = moved if tile is None else jnp.where(lane < width * g, tile, moved)
        out.append(tile)
    return out


def pack_halo(west, east):
    rl = west.shape[0]
    lane = lax.broadcasted_iota(jnp.int32, (rl, LANES), 1)
    small = lax.broadcasted_iota(jnp.int32, (SUB, LANES), 1)
    both = pltpu.roll(jnp.where(lane < LANES // 2, east, west), HALO, 1)
    tile = None
    for q in range(rl // SUB):
        piece = both[q * SUB : (q + 1) * SUB]
        moved = piece if q == 0 else pltpu.roll(piece, 2 * HALO * q, 1)
        tile = moved if tile is None else jnp.where(small < 2 * HALO * q, tile, moved)
    return tile


def pack_kernel(width, s_ref, west_ref, east_ref, send_ref):
    fields, rl, total = s_ref.shape
    tiles = width // LANES
    bands = total // width
    for f in range(fields):
        for i in range(bands):
            lo = i * width
            for h in range(tiles):
                send_ref[i, f, h * rl : (h + 1) * rl, :] = s_ref[f, :, lo + h * LANES : lo + (h + 1) * LANES]
            west = west_ref[f] if i == 0 else s_ref[f, :, lo - LANES : lo]
            east = east_ref[f] if i == bands - 1 else s_ref[f, :, lo + width : lo + width + LANES]
            send_ref[i, f, tiles * rl :, :] = pack_halo(west, east)


def pack_coef_kernel(width, band_ref, m_ref, y_ref, x_ref, coef_ref):
    rl, total = m_ref.shape
    tiles = width // LANES
    band = band_ref[0]
    lo = pl.multiple_of(band * width, LANES)
    lo_w = pl.multiple_of(lax.rem(band * width + (total - LANES), total), LANES)
    lo_e = pl.multiple_of(lax.rem((band + 1) * width, total), LANES)
    for n, ref in enumerate((m_ref, y_ref, x_ref)):
        for h in range(tiles):
            coef_ref[n, h * rl : (h + 1) * rl, :] = ref[:, pl.ds(lo + h * LANES, LANES)]
        coef_ref[n, tiles * rl :, :] = pack_halo(ref[:, pl.ds(lo_w, LANES)], ref[:, pl.ds(lo_e, LANES)])


def unpack_kernel(width, g_ref, out_ref):
    fields, rl, total = out_ref.shape
    for i in range(total // width):
        for f in range(fields):
            for h in range(width // LANES):
                lo = i * width + h * LANES
                out_ref[f, :, lo : lo + LANES] = g_ref[i * fields + f, h * rl : (h + 1) * rl, :]


def finish_coefficients(m, y, x):
    scale = 2.0 / DELTA
    lane = lax.broadcasted_iota(jnp.int32, m.shape, 1)
    south = jnp.where(lane == 0, 0.0, pltpu.roll(y, 1, 1))
    west = pltpu.roll(x, 1, 0)
    diag = scale * (CENTER - m - (y + south) - (x + west))
    return diag, scale * x, scale * y


def coef_kernel(width, times, g_ref, diag_ref, lon_ref, lat_ref, t_ref, tile_ref):
    lats, count, _, _ = g_ref.shape
    tiles = width // LANES
    rl = g_ref.shape[2] * LANES // (width + 2 * HALO)
    for n in range(count):
        for h in range(tiles):
            for l in range(lats):
                tile_ref[l * rl : (l + 1) * rl, :] = g_ref[l, n, h * rl : (h + 1) * rl, :]
            t_ref[n, HALO + h * LANES : HALO + (h + 1) * LANES, :] = tile_ref[...].T
    for l in range(lats):
        got = halo_group([g_ref[l, n, tiles * rl :, :] for n in range(count)], 2 * HALO)
        for q, piece in enumerate(got):
            tile_ref[l * rl + q * SUB : l * rl + (q + 1) * SUB, :] = piece
    turned = tile_ref[...].T
    for n in range(count):
        t_ref[n, :HALO, :] = turned[n * 2 * HALO : n * 2 * HALO + HALO]
        t_ref[n, HALO + width :, :] = turned[n * 2 * HALO + HALO : (n + 1) * 2 * HALO]
    for n, value in enumerate(finish_coefficients(t_ref[0], t_ref[1], t_ref[2])):
        t_ref[n] = value
    rows = t_ref.shape[2]
    groups = LANES // times
    columns = (width + 2 * HALO) // groups
    stride = rows + PAD
    zero = jnp.zeros((PAD, LANES), jnp.float32)
    for c in range(columns):
        for n, ref in enumerate((diag_ref, lon_ref, lat_ref)):
            picked = [t_ref[n, g * columns + c : g * columns + c + 1, :] for g in range(groups)]
            turned = jnp.concatenate([jnp.broadcast_to(row, (times, rows)) for row in picked], 0).T
            if n == 2:
                ref[c * stride : c * stride + PAD, :] = zero
                ref[c * stride + PAD : (c + 1) * stride, :] = turned
            else:
                ref[c * rows : (c + 1) * rows, :] = turned
    lat_ref[columns * stride :, :] = zero


def solve_kernel(width, g_ref, diag_ref, lon_ref, lat_ref, c_ref, out_ref, b_ref, p_ref, q_ref, line_ref, t_ref, tile_ref):
    full = width + 2 * HALO
    times, _, rows = t_ref.shape
    lats = g_ref.shape[0] // times
    tiles = width // LANES
    rl = rows // lats
    groups = LANES // times
    columns = full // groups
    stride = rows + PAD
    for t in range(times):
        for h in range(tiles):
            turned = jnp.concatenate([g_ref[t * lats + l, h * rl : (h + 1) * rl, :] for l in range(lats)], 0).T
            t_ref[t, HALO + h * LANES : HALO + (h + 1) * LANES, :] = turned
    per = LANES // (2 * HALO)
    for g in range(times // per):
        for l in range(lats):
            got = halo_group([g_ref[(g * per + n) * lats + l, tiles * rl :, :] for n in range(per)], 2 * HALO)
            for q, piece in enumerate(got):
                tile_ref[l * rl + q * SUB : l * rl + (q + 1) * SUB, :] = piece
        turned = tile_ref[...].T
        for n in range(per):
            t_ref[g * per + n, :HALO, :] = turned[n * 2 * HALO : n * 2 * HALO + HALO]
            t_ref[g * per + n, HALO + width :, :] = turned[n * 2 * HALO + HALO : (n + 1) * 2 * HALO]

    zero = jnp.zeros((PAD, LANES), jnp.float32)
    for ref in (b_ref, p_ref, q_ref):
        for c in range(columns + 1):
            ref[c * stride : c * stride + PAD, :] = zero

    def to_frequencies(block, carry):
        lo = pl.multiple_of(block * SUB, SUB)
        v = spread([t_ref[t, pl.ds(lo, SUB), :] for t in range(times)])
        for k in range(times):
            line_ref[pl.ds(lo * times + k, SUB, stride=times), :] = v[k]
        return carry

    lax.fori_loop(0, full // SUB, to_frequencies, 0)

    def place(group, column):
        lo = (group * columns + column) * times
        return slice(lo, lo + times)

    for c in range(columns):
        turned = jnp.concatenate([line_ref[place(g, c), :] for g in range(groups)], 0).T
        b_ref[c * stride + PAD : (c + 1) * stride, :] = turned
    run_sweeps(columns, rows, b_ref, p_ref, q_ref, diag_ref, lon_ref, lat_ref, c_ref)
    for c in range(columns):
        turned = p_ref[c * stride + PAD : (c + 1) * stride, :].T
        for g in range(groups):
            line_ref[place(g, c), :] = turned[g * times : (g + 1) * times]

    def to_times(block, carry):
        lo = pl.multiple_of(block * SUB, SUB)
        base = (HALO + lo) * times
        v = gather_times([line_ref[pl.ds(base + k, SUB, stride=times), :] for k in range(times)])
        for t in range(times):
            t_ref[t, pl.ds(lo, SUB), :] = v[t]
        return carry

    lax.fori_loop(0, width // SUB, to_times, 0)
    for t in range(times):
        for h in range(tiles):
            turned = t_ref[t, h * LANES : (h + 1) * LANES, :].T
            for l in range(lats):
                out_ref[t * lats + l, h * rl : (h + 1) * rl, :] = turned[l * rl : (l + 1) * rl]


def sweep_kernel(width, b_ref, diag_ref, lon_ref, lat_ref, c_ref, p_ref, q_ref):
    times = c_ref.shape[0] // (SWEEPS + 1)
    lanes = b_ref.shape[1]

    def rows(j):
        return pl.ds(pl.multiple_of(j * times, SUB), times)

    def wide(ref, j):
        return jnp.broadcast_to(ref[pl.ds(j, 1), :], (times, lanes))

    def begin(j, carry):
        p_ref[rows(j), :] = c_ref[SWEEPS * times :, :] * b_ref[rows(j), :]
        q_ref[rows(j), :] = jnp.zeros((times, lanes), jnp.float32)
        return carry

    lax.fori_loop(0, b_ref.shape[0] // times, begin, 0)

    def sweep(degree, new_ref, old_ref, last=False):
        def step(j, carry):
            j = j + PAD
            near = new_ref[rows(j), :]
            image = wide(diag_ref, j) * near + wide(lon_ref, j) * new_ref[rows(j + 1), :]
            image = image + wide(lon_ref, j - 1) * new_ref[rows(j - 1), :]
            lat = wide(lat_ref, j)
            image = image + lat * pltpu.roll(near, lanes - 1, 1) + pltpu.roll(lat * near, 1, 1)
            older = old_ref[rows(j), :]
            total = c_ref[rows(degree), :] * b_ref[rows(j), :] + image - older
            old_ref[rows(j), :] = total - older if last else total
            return carry

        lax.fori_loop(0, width, step, 0)

    def pair(index, carry):
        sweep(SWEEPS - 1 - 2 * index, p_ref, q_ref)
        sweep(SWEEPS - 2 - 2 * index, q_ref, p_ref)
        return carry

    lax.fori_loop(0, SWEEPS // 2 - 1, pair, 0)
    sweep(1, p_ref, q_ref)
    sweep(0, q_ref, p_ref, True)


VMEM = pl.BlockSpec(memory_space=pltpu.VMEM)
SMEM = pl.BlockSpec(memory_space=pltpu.SMEM)


def params(limit=None):
    return pltpu.CompilerParams(vmem_limit_bytes=limit)


def gather_rows(block, axis):
    count = lax.axis_size(axis)
    me = lax.axis_index(axis)
    got = block[None]
    step = 1
    while step < count:
        other = lax.ppermute(got, axis, [(i, i ^ step) for i in range(count)])
        low = (me & step) == 0
        got = jnp.concatenate([jnp.where(low, got, other), jnp.where(low, other, got)], 0)
        step *= 2
    return got


def solve_packed(states, mass_term, lat_coupling, lon_coupling):
    fields, _, rl, nlon = states.shape
    times, lats = lax.axis_size("tm"), lax.axis_size("lat")
    width = nlon // times
    rows = rl * lats
    full = width + 2 * HALO
    height = full * rl // LANES
    f32 = jnp.float32
    step = PACK_BANDS * width
    tiles = nlon // LANES
    send = pl.pallas_call(
        lambda *refs: pack_kernel(width, *refs),
        grid=(times // PACK_BANDS,),
        out_shape=jax.ShapeDtypeStruct((times, lats, height, LANES), f32),
        in_specs=[
            pl.BlockSpec((fields, rl, step), lambda i: (0, 0, i)),
            pl.BlockSpec((fields, rl, LANES), lambda i: (0, 0, (i * (step // LANES) + tiles - 1) % tiles)),
            pl.BlockSpec((fields, rl, LANES), lambda i: (0, 0, ((i + 1) * (step // LANES)) % tiles)),
        ],
        out_specs=pl.BlockSpec((PACK_BANDS, lats, height, LANES), lambda i: (i, 0, 0, 0)),
        cost_estimate=pl.CostEstimate(flops=0, transcendentals=0, bytes_accessed=8 * states.size),
        compiler_params=params(16 << 20),
        name="pack",
    )(*[states.reshape(fields, rl, nlon)] * 3)
    band = lax.axis_index("tm").astype(jnp.int32).reshape(1)
    coef = pl.pallas_call(
        lambda *refs: pack_coef_kernel(width, *refs),
        out_shape=jax.ShapeDtypeStruct((3, height, LANES), f32),
        in_specs=[SMEM] + [VMEM] * 3,
        out_specs=VMEM,
        cost_estimate=pl.CostEstimate(flops=0, transcendentals=0, bytes_accessed=16 * mass_term.size),
        compiler_params=params(16 << 20),
        name="pack_coefficients",
    )(band, mass_term, lat_coupling, lon_coupling)
    coefs = gather_rows(coef, "lat")
    got = lax.all_to_all(send.reshape(times * lats, height, LANES), ("tm", "lat"), 0, 0, tiled=True)
    groups = LANES // times
    columns = full // groups
    slab = ((rows + PAD) * columns + PAD, LANES)
    flat = (rows * columns, LANES)
    diag, lon, lat = pl.pallas_call(
        lambda *refs: coef_kernel(width, times, *refs),
        out_shape=(jax.ShapeDtypeStruct(flat, f32),) * 2 + (jax.ShapeDtypeStruct(slab, f32),),
        in_specs=[VMEM],
        out_specs=(VMEM,) * 3,
        scratch_shapes=[pltpu.VMEM((3, full, rows), f32), pltpu.VMEM((rows, LANES), f32)],
        cost_estimate=pl.CostEstimate(flops=30 * full * rows, transcendentals=0, bytes_accessed=128 * full * rows),
        compiler_params=params(16 << 20),
        name="coefficients",
    )(coefs)
    basis = time_basis(times)
    scale = np.max(np.abs(basis), 1) ** 2
    scale = np.where(scale > 1.5 / times, 2.0 / times, 1.0 / times)
    c_rows = jnp.asarray(np.tile(weights(times) * scale[None, :], (1, groups)), f32)
    out = pl.pallas_call(
        lambda *refs: solve_kernel(width, *refs),
        out_shape=jax.ShapeDtypeStruct((times * lats, width * rl // LANES, LANES), f32),
        in_specs=[VMEM] * 5,
        out_specs=VMEM,
        scratch_shapes=[pltpu.VMEM(slab, f32)] * 3
        + [pltpu.VMEM((full * times, rows), f32), pltpu.VMEM((times, full, rows), f32), pltpu.VMEM((rows, LANES), f32)],
        cost_estimate=pl.CostEstimate(
            flops=12 * SWEEPS * full * times * rows, transcendentals=0, bytes_accessed=8 * full * times * rows
        ),
        compiler_params=params(24 << 20),
        name="solve",
    )(got, diag, lon, lat, c_rows)
    back = lax.all_to_all(out, ("tm", "lat"), 0, 0, tiled=True)
    result = pl.pallas_call(
        lambda *refs: unpack_kernel(width, *refs),
        out_shape=jax.ShapeDtypeStruct((fields, rl, nlon), f32),
        in_specs=[VMEM],
        out_specs=VMEM,
        cost_estimate=pl.CostEstimate(flops=0, transcendentals=0, bytes_accessed=8 * states.size),
        compiler_params=params(16 << 20),
        name="unpack",
    )(back)
    return result.reshape(states.shape)


def solve_general(states, mass_term, lat_coupling, lon_coupling):
    fields, tl, rl, nlon = states.shape
    tm, lats = lax.axis_size("tm"), lax.axis_size("lat")
    times, rows, parts = tl * tm, rl * lats, lats // fields
    width = nlon // (tm * parts)
    full = width + 2 * HALO
    length = padded_length(full)
    f32 = jnp.float32

    def wrapped(a):
        return jnp.concatenate([a[..., nlon - HALO :], a, a[..., :HALO]], -1)

    wide = wrapped(states)
    bands = jnp.stack([wide[..., n * width : n * width + full] for n in range(tm * parts)])
    bands = bands.reshape(tm, parts, fields, tl, rl, full).transpose(0, 2, 1, 3, 4, 5)
    got = lax.all_to_all(bands.reshape(tm * lats, tl, rl, full), ("tm", "lat"), 0, 0, tiled=True)
    field = got.reshape(tm, lats, tl, rl, full).transpose(4, 0, 2, 1, 3).reshape(full, times, rows)
    basis = jnp.asarray(time_basis(times), f32)
    b = jnp.einsum("kt,jtr->jkr", basis, field, precision=lax.Precision.HIGHEST)
    coef = wrapped(jnp.stack([mass_term, lat_coupling, lon_coupling]))
    first = lax.axis_index("tm") * parts
    mine = jnp.stack([lax.dynamic_slice_in_dim(coef, (first + n) * width, full, 2) for n in range(parts)])
    mine = jnp.broadcast_to(mine[None], (fields,) + mine.shape).reshape(lats, 3, rl, full)
    all_rows = lax.all_to_all(mine, "lat", 0, 0, tiled=True)
    m, y, x = all_rows.transpose(1, 3, 0, 2).reshape(3, full, rows)
    scale = 2.0 / DELTA
    south = jnp.concatenate([jnp.zeros((full, 1), f32), y[:, :-1]], 1)
    diag = scale * (CENTER - m - (y + south) - (x + jnp.roll(x, 1, 0)))
    lat = scale * jnp.concatenate([y[:, :-1], jnp.zeros((full, 1), f32)], 1)
    ends = ((PAD, length - PAD - full), (0, 0))
    diag, lon, lat = (jnp.pad(a, ends) for a in (diag, scale * x, lat))
    b = jnp.pad(b, (ends[0], (0, 0), (0, 0))).reshape(length * times, rows)
    c = weights(times)
    c_rows = jnp.broadcast_to(jnp.asarray(c.reshape(-1, 1), f32), ((SWEEPS + 1) * times, rows))
    slab = pltpu.VMEM((length * times, rows), f32)
    solved = pl.pallas_call(
        lambda *refs: sweep_kernel(full, *refs),
        out_shape=jax.ShapeDtypeStruct((length * times, rows), f32),
        in_specs=[VMEM] * 5,
        out_specs=VMEM,
        scratch_shapes=[slab],
        name="sweeps",
    )(b, diag, lon, lat, c_rows)
    solved = solved.reshape(length, times, rows)[PAD + HALO : PAD + HALO + width]
    field = jnp.einsum("kt,jkr->jtr", basis, solved, precision=lax.Precision.HIGHEST)
    field = field.reshape(width, tm, tl, lats, rl).transpose(1, 3, 2, 4, 0).reshape(tm * lats, tl, rl, width)
    back = lax.all_to_all(field, ("tm", "lat"), 0, 0, tiled=True)
    back = back.reshape(tm, fields, parts, tl, rl, width).transpose(1, 3, 4, 0, 2, 5)
    return back.reshape(fields, tl, rl, nlon)


def per_device(states, mass_term, lat_coupling, lon_coupling):
    fields, tl, rl, nlon = states.shape
    tm, lats = lax.axis_size("tm"), lax.axis_size("lat")
    packed = tl == 1 and tm == SUB and lats == fields and rl * lats == LANES
    packed = packed and nlon % (tm * LANES) == 0 and 2 * HALO * rl == SUB * LANES
    packed = packed and (nlon // tm + 2 * HALO) % (LANES // tm) == 0 and tm % PACK_BANDS == 0
    plan = solve_packed if packed else solve_general
    return plan(states, mass_term, lat_coupling, lon_coupling)


def solution(mesh):
    placed = (P(None, "tm", "lat", None), P("lat", None), P("lat", None), P("lat", None))
    return jax.shard_map(
        per_device,
        mesh=mesh,
        in_specs=placed,
        out_specs=P(None, "tm", "lat", None),
        check_vma=False,
    )
```

time: 98.1 us -> 85 us (0.87)
  Pallas kernels: 29.7 us -> 16.2 us
  local copies, waits for them, and re-layouts: 3.68 us -> 5.82 us
    pallas_call x3 -> x5, Pallas kernels: 29.7 us -> 16.2 us  [the longest x1 11.5 us: solve_packed(): pl.pallas_call(lambda *refs: solve_kernel(width, *refs), out_shape=jax.Sh...]
    unnamed x6 -> x18, local copies, waits for them, and re-layouts: 0.23 us -> 5.82 us
    reshape x1 -> x0, local copies, waits for them, and re-layouts: 1.81 us -> none  [solve_packed(): return back.transpose(1, 3, 0, 2, 4).reshape(fields, 1, rl, nlon)]
  transfers between devices with their start and end apart: 3 -> 3, of which waited for: 3 -> 3; matrix products, arithmetic and copies ran while one was open for 1% -> 0% of each run, Pallas kernels for 2% -> 2%
where the time goes in v1:
time: 85 us; the launch traced here: 84.7 us
  blocking collectives  29.9 us (35%)
  waiting for transfers between devices  23 us (27%)
  Pallas kernels  16.2 us (19%)
  starting transfers between devices  9.67 us (11%)
  local copies, waits for them, and re-layouts  5.82 us (7%)
    all_to_all x1, blocking collectives, solve_packed(): back = lax.all_to_all(out, ('tm', 'lat'), 0, 0, tiled=True)  29.9 us
    ppermute x2, waiting for transfers between devices, gather_rows(): other = lax.ppermute(got, axis, [(i, i ^ step) for i in range(count)])  20 us
    pallas_call x1, Pallas kernels, solve_packed(): pl.pallas_call(lambda *refs: solve_kernel(width, *refs), out_shape=jax.Sh...  11.5 us
    all_to_all x1, starting transfers between devices, solve_packed(): lax.all_to_all(send.reshape(times * lats, height, LANES), ('tm', 'lat'),...  7.33 us
    unnamed x18, local copies, waits for them, and re-layouts  5.82 us
    all_to_all x1, waiting for transfers between devices, solve_packed(): lax.all_to_all(send.reshape(times * lats, height, LANES), ('tm', 'lat'),...  3.01 us
    ppermute x2, starting transfers between devices, gather_rows(): other = lax.ppermute(got, axis, [(i, i ^ step) for i in range(count)])  2.35 us
    pallas_call x1, Pallas kernels, solve_packed(): pl.pallas_call(lambda *refs: pack_kernel(width, *refs), grid=(times // PA...  2.1 us
  transfers between devices with their start and end apart: 3, of which 3 were waited for; matrix products, arithmetic and copies ran while one was open for 0% of the time, Pallas kernels for 2%

profile of v1, /device:TPU:0, one launch (start us, length us, event | category | flops | bytes accessed | tf_op | source)
XLA Modules:
  0.0 84.7 jit_solution(12492205515239776092)
XLA Ops:
  0.0 0.0 copy-start
  0.0 1.2 %copy-done = f32[4,1,32,2048]{3,2,1,0:T(8,128)S(1)} copy-done((f32[4,1,32,2048]{3,2,1,0:T(8,128)S(1)}, f32[4,1,32,2048]{3,2,1,0:T(8,128)}, u32[]{:S(2)}) %copy-start) | copy-done | bytes 1048600
  1.2 2.1 %pack.1 = f32[8,4,72,128]{3,2,1,0:T(8,128)} custom-call(f32[4,32,2048]{2,1,0:T(8,128)S(1)} %bitcast.9, f32[4,32,2048]{2,1,0:T(8,128)S(1)} %bitcast.10, f32[4,32,2048]{2,1,0:T(8,128)S(1)} %bitcast.11), custom_call_target="tpu_custom_call" | custom-call | bytes 2097152 | tf_op jit(solution)/shard_map/pack/pallas_call | solution.py:374
  3.3 0.0 copy-start.5
  3.3 0.0 copy-start.6
  3.3 0.0 copy-start.7
  3.3 7.3 %all-to-all-start = ((f32[32,72,128]{2,1,0:T(8,128)}), f32[32,72,128]{2,1,0:T(8,128)S(1)}, u32[]{:S(2)}, u32[]{:S(2)}) async-start(f32[32,72,128]{2,1,0:T(8,128)} %bitcast.1), calls=%async_computation | async-start | bytes 2359296 | tf_op jit(solution)/shard_map/all_to_all | solution.py:399
  10.7 0.0 copy-done.5
  10.7 0.0 copy-done.6
  10.7 0.0 copy-done.7
  10.7 0.2 pack_coefficients.1
  10.9 1.8 %collective-permute-start = (f32[1,3,72,128]{3,2,1,0:T(8,128)S(1)}, f32[1,3,72,128]{3,2,1,0:T(8,128)S(1)}, u32[]{:S(2)}, u32[]{:S(2)}) collective-permute-start(f32[1,3,72,128]{3,2,1,0:T(8,128)S(1)} %bitcast.12), channel_id=1, source_target_pairs={{0,1},{1,0},{2,3},{3,2},{4,5},{5,4},{6,7},{7,6},{8,9},{9,8},{10,11... | collective-permute-start | bytes 331784 | tf_op jit(solution)/shard_map/ppermute | solution.py:357
  12.7 11.8 %collective-permute-done = f32[1,3,72,128]{3,2,1,0:T(8,128)S(1)} collective-permute-done((f32[1,3,72,128]{3,2,1,0:T(8,128)S(1)}, f32[1,3,72,128]{3,2,1,0:T(8,128)S(1)}, u32[]{:S(2)}, u32[]{:S(2)}) %collective-permute-start) | collective-permute-done | bytes 110624 | tf_op jit(solution)/shard_map/ppermute | solution.py:357
  24.5 0.0 copy-start.8
  24.5 0.5 collective-permute-start.1
  25.1 8.2 %collective-permute-done.1 = f32[2,3,72,128]{3,2,1,0:T(8,128)S(1)} collective-permute-done((f32[2,3,72,128]{3,2,1,0:T(8,128)S(1)}, f32[2,3,72,128]{3,2,1,0:T(8,128)S(1)}, u32[]{:S(2)}, u32[]{:S(2)}) %collective-permute-start.1) | collective-permute-done | bytes 221216 | tf_op jit(solution)/shard_map/ppermute | solution.py:357
  33.3 1.4 %coefficients.1 = (f32[2304,128]{1,0:T(8,128)S(1)}, f32[2304,128]{1,0:T(8,128)S(1)}, f32[2456,128]{1,0:T(8,128)S(1)}) custom-call(f32[4,3,72,128]{3,2,1,0:T(8,128)S(1)} %pad_maximum_fusion.refs_0_), custom_call_target="tpu_custom_call" | custom-call | flops 1105920 | bytes 4718592 | tf_op jit(solution)/shard_map/coefficients/pallas_call | solution.py:404
  34.7 0.0 copy-start.1
  34.7 1.0 %copy-done.1 = f32[2304,128]{1,0:T(8,128)} copy-done((f32[2304,128]{1,0:T(8,128)}, f32[2304,128]{1,0:T(8,128)S(1)}, u32[]{:S(2)}) %copy-start.1) | copy-done | bytes 1179672
  35.7 0.0 copy-start.3
  35.7 1.0 %copy-done.3 = f32[2304,128]{1,0:T(8,128)} copy-done((f32[2304,128]{1,0:T(8,128)}, f32[2304,128]{1,0:T(8,128)S(1)}, u32[]{:S(2)}) %copy-start.3) | copy-done | bytes 1179672
  36.7 3.0 %all-to-all-done.refs_0_ = f32[32,72,128]{2,1,0:T(8,128)S(1)} async-done(((f32[32,72,128]{2,1,0:T(8,128)}), f32[32,72,128]{2,1,0:T(8,128)S(1)}, u32[]{:S(2)}, u32[]{:S(2)}) %all-to-all-start) | async-done | bytes 1179680 | tf_op jit(solution)/shard_map/all_to_all | solution.py:399
  39.7 0.0 copy-done.8
  39.8 0.0 copy-start.2
  39.8 1.3 %copy-done.2 = f32[2304,128]{1,0:T(8,128)S(1)} copy-done((f32[2304,128]{1,0:T(8,128)S(1)}, f32[2304,128]{1,0:T(8,128)}, u32[]{:S(2)}) %copy-start.2) | copy-done | bytes 1179672
  41.0 0.0 copy-start.4
  41.0 1.3 %copy-done.4 = f32[2304,128]{1,0:T(8,128)S(1)} copy-done((f32[2304,128]{1,0:T(8,128)S(1)}, f32[2304,128]{1,0:T(8,128)}, u32[]{:S(2)}) %copy-start.4) | copy-done | bytes 1179672
  42.3 11.5 %solve.1 = f32[32,64,128]{2,1,0:T(8,128)S(1)} custom-call(f32[32,72,128]{2,1,0:T(8,128)S(1)} %all-to-all-done.refs_0_, f32[2304,128]{1,0:T(8,128)S(1)} %copy-done.2, f32[2304,128]{1,0:T(8,128)S(1)} %copy-done.4, f32[2456,128]{1,0:T(8,128)S(1)} %get-tuple-element.10.refs_3_, f32[17,128]{1,0:T(8,128)S(1)} %copy-done.8), custom_call_target="tpu_custom_call" | custom-call | flops 56623104 | bytes 2359296 | tf_op jit(solution)/shard_map/solve/pallas_call | solution.py:418
  53.8 29.9 %all_to_all.10.refs_0_ = f32[32,64,128]{2,1,0:T(8,128)S(1)} all-to-all(f32[32,64,128]{2,1,0:T(8,128)S(1)} %solve.1), channel_id=1, replica_groups=mesh['tm'=8,'lat'=4] {'tm','lat'}, dimensions={0} | all-to-all | bytes 2097152 | tf_op jit(solution)/shard_map/all_to_all | solution.py:431
  83.7 1.1 %unpack.1 = f32[4,32,2048]{2,1,0:T(8,128)} custom-call(f32[32,64,128]{2,1,0:T(8,128)S(1)} %all_to_all.10.refs_0_), custom_call_target="tpu_custom_call" | custom-call | bytes 2097152 | tf_op jit(solution)/shard_map/unpack/pallas_call | solution.py:432
  (4 shorter events, 0.1 us)
Async XLA Ops:
  0.0 1.2 %copy-start = (f32[4,1,32,2048]{3,2,1,0:T(8,128)S(1)}, f32[4,1,32,2048]{3,2,1,0:T(8,128)}, u32[]{:S(2)}) copy-start(f32[4,1,32,2048]{3,2,1,0:T(8,128)} %param.5) | copy-start | bytes 3145732
  3.3 7.3 %copy-start.5 = (f32[32,2048]{1,0:T(8,128)S(1)}, f32[32,2048]{1,0:T(8,128)}, u32[]{:S(2)}) copy-start(f32[32,2048]{1,0:T(8,128)} %refs_1_.1) | copy-start | bytes 786436
  3.3 7.4 %copy-start.6 = (f32[32,2048]{1,0:T(8,128)S(1)}, f32[32,2048]{1,0:T(8,128)}, u32[]{:S(2)}) copy-start(f32[32,2048]{1,0:T(8,128)} %refs_2_.1) | copy-start | bytes 786436
  3.3 7.4 %copy-start.7 = (f32[32,2048]{1,0:T(8,128)S(1)}, f32[32,2048]{1,0:T(8,128)}, u32[]{:S(2)}) copy-start(f32[32,2048]{1,0:T(8,128)} %refs_3_.1) | copy-start | bytes 786436
  3.3 36.4 %all-to-all-start = ((f32[32,72,128]{2,1,0:T(8,128)}), f32[32,72,128]{2,1,0:T(8,128)S(1)}, u32[]{:S(2)}, u32[]{:S(2)}) async-start(f32[32,72,128]{2,1,0:T(8,128)} %bitcast.1), calls=%async_computation | async-start | bytes 2359296 | tf_op jit(solution)/shard_map/all_to_all | solution.py:399
  10.9 13.6 %collective-permute-start = (f32[1,3,72,128]{3,2,1,0:T(8,128)S(1)}, f32[1,3,72,128]{3,2,1,0:T(8,128)S(1)}, u32[]{:S(2)}, u32[]{:S(2)}) collective-permute-start(f32[1,3,72,128]{3,2,1,0:T(8,128)S(1)} %bitcast.12), channel_id=1, source_target_pairs={{0,1},{1,0},{2,3},{3,2},{4,5},{5,4},{6,7},{7,6},{8,9},{9,8},{10,11... | collective-permute-start | bytes 331784 | tf_op jit(solution)/shard_map/ppermute | solution.py:357
  24.5 15.2 %copy-start.8 = (f32[17,128]{1,0:T(8,128)S(1)}, f32[17,128]{1,0:T(8,128)}, u32[]{:S(2)}) copy-start(f32[17,128]{1,0:T(8,128)} %constant.17.clone.refs_4_) | copy-start | bytes 26116
  24.5 8.7 %collective-permute-start.1 = (f32[2,3,72,128]{3,2,1,0:T(8,128)S(1)}, f32[2,3,72,128]{3,2,1,0:T(8,128)S(1)}, u32[]{:S(2)}, u32[]{:S(2)}) collective-permute-start(f32[2,3,72,128]{3,2,1,0:T(8,128)S(1)} %pad_maximum_fusion.1), channel_id=1, source_target_pairs={{0,2},{1,3},{2,0},{3,1},{4,6},{5,7},{6,4},{7,5},{8,10},{9,11},{10,... | collective-permute-start | bytes 663560 | tf_op jit(solution)/shard_map/ppermute | solution.py:357
  34.7 1.0 %copy-start.1 = (f32[2304,128]{1,0:T(8,128)}, f32[2304,128]{1,0:T(8,128)S(1)}, u32[]{:S(2)}) copy-start(f32[2304,128]{1,0:T(8,128)S(1)} %get-tuple-element.8.refs_1_) | copy-start | bytes 3538948
  35.7 1.0 %copy-start.3 = (f32[2304,128]{1,0:T(8,128)}, f32[2304,128]{1,0:T(8,128)S(1)}, u32[]{:S(2)}) copy-start(f32[2304,128]{1,0:T(8,128)S(1)} %get-tuple-element.9.refs_2_) | copy-start | bytes 3538948
  39.8 1.3 %copy-start.2 = (f32[2304,128]{1,0:T(8,128)S(1)}, f32[2304,128]{1,0:T(8,128)}, u32[]{:S(2)}) copy-start(f32[2304,128]{1,0:T(8,128)} %copy-done.1) | copy-start | bytes 3538948
  41.0 1.3 %copy-start.4 = (f32[2304,128]{1,0:T(8,128)S(1)}, f32[2304,128]{1,0:T(8,128)}, u32[]{:S(2)}) copy-start(f32[2304,128]{1,0:T(8,128)} %copy-done.3) | copy-start | bytes 3538948

commit v2 on v1

--- a/solution.py
+++ b/solution.py
@@ -10,7 +10,7 @@
 
 SWEEPS = 16
 HALO = SWEEPS
-PACK_BANDS = 2
+BAND_TURNS = (0, 2, 4, 6, 1, 3, 5, 7)
 PAD = 8
 LANES = 128
 SUB = 8
@@ -150,40 +150,96 @@
     return tile
 
 
-def pack_kernel(width, s_ref, west_ref, east_ref, send_ref):
-    fields, rl, total = s_ref.shape
-    tiles = width // LANES
+def relative(place, turn):
+    return lax.bitwise_xor(place, jnp.int32(turn))
+
+
+def pack_kernel(here_ref, s_ref, *refs):
+    coef_refs, early_ref, late_refs = refs[:3], refs[3], refs[4:8]
+    s_v, e_v, l_v, west_v, near_v, east_v, c_v, s_sem, c_sem, e_sem, l_sem = refs[8:]
+    rl, total = s_ref.shape[1:]
+    width = 2 * LANES
     bands = total // width
-    for f in range(fields):
+    lane = lax.broadcasted_iota(jnp.int32, (rl, LANES), 1)
+    order = [1, 2, 3, 0]
+    loads = {r: pltpu.make_async_copy(s_ref.at[relative(here_ref[1], r)], s_v.at[r], s_sem.at[r]) for r in order}
+    band = here_ref[0]
+    starts = [lax.rem(band * width + (total - LANES), total), band * width, lax.rem((band + 1) * width, total)]
+    starts = [pl.multiple_of(start, LANES) for start in starts]
+    pieces = []
+    for n, ref in enumerate(coef_refs):
+        for k, (start, v) in enumerate(zip(starts, (west_v, near_v, east_v))):
+            part = ref.at[:, pl.ds(start, v.shape[2])]
+            pieces.append(pltpu.make_async_copy(part, v.at[n], c_sem.at[n * 3 + k]))
+    loads[order[0]].start()
+    for piece in pieces:
+        piece.start()
+    for r in order[1:]:
+        loads[r].start()
+    for place, r in enumerate(order):
+        loads[r].wait()
         for i in range(bands):
             lo = i * width
-            for h in range(tiles):
-                send_ref[i, f, h * rl : (h + 1) * rl, :] = s_ref[f, :, lo + h * LANES : lo + (h + 1) * LANES]
-            west = west_ref[f] if i == 0 else s_ref[f, :, lo - LANES : lo]
-            east = east_ref[f] if i == bands - 1 else s_ref[f, :, lo + width : lo + width + LANES]
-            send_ref[i, f, tiles * rl :, :] = pack_halo(west, east)
-
-
-def pack_coef_kernel(width, band_ref, m_ref, y_ref, x_ref, coef_ref):
-    rl, total = m_ref.shape
-    tiles = width // LANES
-    band = band_ref[0]
-    lo = pl.multiple_of(band * width, LANES)
-    lo_w = pl.multiple_of(lax.rem(band * width + (total - LANES), total), LANES)
-    lo_e = pl.multiple_of(lax.rem((band + 1) * width, total), LANES)
-    for n, ref in enumerate((m_ref, y_ref, x_ref)):
-        for h in range(tiles):
-            coef_ref[n, h * rl : (h + 1) * rl, :] = ref[:, pl.ds(lo + h * LANES, LANES)]
-        coef_ref[n, tiles * rl :, :] = pack_halo(ref[:, pl.ds(lo_w, LANES)], ref[:, pl.ds(lo_e, LANES)])
-
-
-def unpack_kernel(width, g_ref, out_ref):
-    fields, rl, total = out_ref.shape
+            west = (lo - LANES) % total
+            after = (lo + width) % total
+            near, far = s_v[r, :, lo : lo + LANES], s_v[r, :, lo + LANES : lo + width]
+            e_v[r, i, :rl, :] = near
+            e_v[r, i, rl:, :] = pack_halo(s_v[r, :, west : west + LANES], far)
+            turn = relative(here_ref[0], i)
+            row = ((turn & 1) * (bands // 2) + lax.shift_right_logical(turn, 1)) * rl
+            both = jnp.where(lane < HALO, s_v[r, :, after : after + LANES], far)
+            l_v[r, pl.ds(pl.multiple_of(row, SUB), rl), :] = pltpu.roll(both, LANES - HALO, 1)
+        pltpu.make_async_copy(l_v.at[r], late_refs[r].at[: bands * rl], l_sem.at[r]).start()
+        pltpu.make_async_copy(e_v.at[r], early_ref.at[:, relative(here_ref[1], r)], e_sem.at[r]).start()
+        if place == 0:
+            for piece in pieces:
+                piece.wait()
+            height = c_v.shape[0] // 3
+            for n in range(3):
+                lo = n * height
+                for h in range(2):
+                    c_v[lo + h * rl : lo + (h + 1) * rl, :] = near_v[n, :, h * LANES : (h + 1) * LANES]
+                c_v[lo + 2 * rl : lo + height, :] = pack_halo(west_v[n], east_v[n])
+            for r2 in order:
+                pltpu.make_async_copy(c_v, late_refs[r2].at[bands * rl :], l_sem.at[len(order) + r2]).start()
+    for r in order:
+        pltpu.make_async_copy(l_v.at[r], late_refs[r].at[: bands * rl], l_sem.at[r]).wait()
+        pltpu.make_async_copy(e_v.at[r], early_ref.at[:, relative(here_ref[1], r)], e_sem.at[r]).wait()
+        pltpu.make_async_copy(c_v, late_refs[r].at[bands * rl :], l_sem.at[len(order) + r]).wait()
+
+
+def unpack_kernel(here_ref, g_ref, *refs):
+    out_ref = refs[-1]
+    fields, _, total = out_ref.shape
+    width = 2 * LANES
     for i in range(total // width):
+        band = relative(here_ref[0], BAND_TURNS[i])
+        lo = pl.multiple_of(band * width, LANES)
         for f in range(fields):
-            for h in range(width // LANES):
-                lo = i * width + h * LANES
-                out_ref[f, :, lo : lo + LANES] = g_ref[i * fields + f, h * rl : (h + 1) * rl, :]
+            out_ref[f, :, i * width + LANES : (i + 1) * width] = g_ref[i * fields + f]
+            out_ref[relative(here_ref[1], f), :, pl.ds(lo, LANES)] = refs[f][i]
+
+
+def moving(plan):
+    def kernel(ins, outs, *refs):
+        for target, at, source, of in plan:
+            refs[ins + target][at] = refs[source][of]
+
+    return kernel
+
+
+def shuffle(plan, arrays, shapes):
+    kernel = moving(plan)
+    count = len(arrays)
+    size = sum(math.prod(shape) for shape in shapes)
+    return pl.pallas_call(
+        lambda *refs: kernel(count, len(shapes), *refs),
+        out_shape=tuple(jax.ShapeDtypeStruct(shape, jnp.float32) for shape in shapes),
+        in_specs=[VMEM] * count,
+        out_specs=(VMEM,) * len(shapes),
+        cost_estimate=pl.CostEstimate(flops=0, transcendentals=0, bytes_accessed=8 * size),
+        compiler_params=params(16 << 20),
+    )(*arrays)
 
 
 def finish_coefficients(m, y, x):
@@ -195,85 +251,58 @@
     return diag, scale * x, scale * y
 
 
-def coef_kernel(width, times, g_ref, diag_ref, lon_ref, lat_ref, t_ref, tile_ref):
-    lats, count, _, _ = g_ref.shape
+def coef_kernel(first, here_ref, g0, g1, g2, g3, diag_ref, lon_ref, lat_ref, t_ref, tile_ref):
+    count, full, rows = t_ref.shape
+    width = full - 2 * HALO
+    received = (g0, g1, g2, g3)
+    rl = rows // len(received)
+    height = full * rl // LANES
     tiles = width // LANES
-    rl = g_ref.shape[2] * LANES // (width + 2 * HALO)
+
+    def block(r, shift=0):
+        return pl.multiple_of(relative(here_ref[1], r) * rl + shift, SUB)
+
     for n in range(count):
         for h in range(tiles):
-            for l in range(lats):
-                tile_ref[l * rl : (l + 1) * rl, :] = g_ref[l, n, h * rl : (h + 1) * rl, :]
+            for r, g_ref in enumerate(received):
+                lo = first + n * height + h * rl
+                tile_ref[pl.ds(block(r), rl), :] = g_ref[lo : lo + rl, :]
             t_ref[n, HALO + h * LANES : HALO + (h + 1) * LANES, :] = tile_ref[...].T
-    for l in range(lats):
-        got = halo_group([g_ref[l, n, tiles * rl :, :] for n in range(count)], 2 * HALO)
+    for r, g_ref in enumerate(received):
+        lows = [first + n * height + tiles * rl for n in range(count)]
+        got = halo_group([g_ref[lo : lo + SUB, :] for lo in lows], 2 * HALO)
         for q, piece in enumerate(got):
-            tile_ref[l * rl + q * SUB : l * rl + (q + 1) * SUB, :] = piece
+            tile_ref[pl.ds(block(r, q * SUB), SUB), :] = piece
     turned = tile_ref[...].T
     for n in range(count):
         t_ref[n, :HALO, :] = turned[n * 2 * HALO : n * 2 * HALO + HALO]
         t_ref[n, HALO + width :, :] = turned[n * 2 * HALO + HALO : (n + 1) * 2 * HALO]
-    for n, value in enumerate(finish_coefficients(t_ref[0], t_ref[1], t_ref[2])):
-        t_ref[n] = value
-    rows = t_ref.shape[2]
+    for ref, value in zip((diag_ref, lon_ref, lat_ref), finish_coefficients(t_ref[0], t_ref[1], t_ref[2])):
+        ref[...] = value
+
+
+def solve_columns(first, coefs, c_ref, p_ref, work, line_ref):
+    b_ref, q_ref, diag_ref, lon_ref, lat_ref = work
+    rows = line_ref.shape[1]
+    times = SUB
     groups = LANES // times
-    columns = (width + 2 * HALO) // groups
+    columns = line_ref.shape[0] // LANES
     stride = rows + PAD
     zero = jnp.zeros((PAD, LANES), jnp.float32)
-    for c in range(columns):
-        for n, ref in enumerate((diag_ref, lon_ref, lat_ref)):
-            picked = [t_ref[n, g * columns + c : g * columns + c + 1, :] for g in range(groups)]
-            turned = jnp.concatenate([jnp.broadcast_to(row, (times, rows)) for row in picked], 0).T
-            if n == 2:
-                ref[c * stride : c * stride + PAD, :] = zero
-                ref[c * stride + PAD : (c + 1) * stride, :] = turned
-            else:
-                ref[c * rows : (c + 1) * rows, :] = turned
-    lat_ref[columns * stride :, :] = zero
-
-
-def solve_kernel(width, g_ref, diag_ref, lon_ref, lat_ref, c_ref, out_ref, b_ref, p_ref, q_ref, line_ref, t_ref, tile_ref):
-    full = width + 2 * HALO
-    times, _, rows = t_ref.shape
-    lats = g_ref.shape[0] // times
-    tiles = width // LANES
-    rl = rows // lats
-    groups = LANES // times
-    columns = full // groups
-    stride = rows + PAD
-    for t in range(times):
-        for h in range(tiles):
-            turned = jnp.concatenate([g_ref[t * lats + l, h * rl : (h + 1) * rl, :] for l in range(lats)], 0).T
-            t_ref[t, HALO + h * LANES : HALO + (h + 1) * LANES, :] = turned
-    per = LANES // (2 * HALO)
-    for g in range(times // per):
-        for l in range(lats):
-            got = halo_group([g_ref[(g * per + n) * lats + l, tiles * rl :, :] for n in range(per)], 2 * HALO)
-            for q, piece in enumerate(got):
-                tile_ref[l * rl + q * SUB : l * rl + (q + 1) * SUB, :] = piece
-        turned = tile_ref[...].T
-        for n in range(per):
-            t_ref[g * per + n, :HALO, :] = turned[n * 2 * HALO : n * 2 * HALO + HALO]
-            t_ref[g * per + n, HALO + width :, :] = turned[n * 2 * HALO + HALO : (n + 1) * 2 * HALO]
-
-    zero = jnp.zeros((PAD, LANES), jnp.float32)
-    for ref in (b_ref, p_ref, q_ref):
+    for ref in (b_ref, p_ref, q_ref, lat_ref):
         for c in range(columns + 1):
             ref[c * stride : c * stride + PAD, :] = zero
-
-    def to_frequencies(block, carry):
-        lo = pl.multiple_of(block * SUB, SUB)
-        v = spread([t_ref[t, pl.ds(lo, SUB), :] for t in range(times)])
-        for k in range(times):
-            line_ref[pl.ds(lo * times + k, SUB, stride=times), :] = v[k]
-        return carry
-
-    lax.fori_loop(0, full // SUB, to_frequencies, 0)
 
     def place(group, column):
         lo = (group * columns + column) * times
         return slice(lo, lo + times)
 
     for c in range(columns):
+        for ref, out_ref in zip(coefs, (diag_ref, lon_ref, lat_ref)):
+            picked = [ref[first + g * columns + c : first + g * columns + c + 1, :] for g in range(groups)]
+            turned = jnp.concatenate([jnp.broadcast_to(row, (times, rows)) for row in picked], 0).T
+            lo = c * stride + PAD if out_ref is lat_ref else c * rows
+            out_ref[lo : lo + rows, :] = turned
         turned = jnp.concatenate([line_ref[place(g, c), :] for g in range(groups)], 0).T
         b_ref[c * stride + PAD : (c + 1) * stride, :] = turned
     run_sweeps(columns, rows, b_ref, p_ref, q_ref, diag_ref, lon_ref, lat_ref, c_ref)
@@ -282,7 +311,24 @@
         for g in range(groups):
             line_ref[place(g, c), :] = turned[g * times : (g + 1) * times]
 
-    def to_times(block, carry):
+
+def to_frequencies(t_ref, line_ref, first):
+    times = t_ref.shape[0]
+
+    def step(block, carry):
+        lo = pl.multiple_of(block * SUB, SUB)
+        v = spread([t_ref[t, pl.ds(lo, SUB), :] for t in range(times)])
+        for k in range(times):
+            line_ref[pl.ds(lo * times + k, SUB, stride=times), :] = v[k]
+        return carry
+
+    lax.fori_loop(first // SUB, t_ref.shape[1] // SUB, step, 0)
+
+
+def to_times(line_ref, t_ref):
+    times = t_ref.shape[0]
+
+    def step(block, carry):
         lo = pl.multiple_of(block * SUB, SUB)
         base = (HALO + lo) * times
         v = gather_times([line_ref[pl.ds(base + k, SUB, stride=times), :] for k in range(times)])
@@ -290,12 +336,56 @@
             t_ref[t, pl.ds(lo, SUB), :] = v[t]
         return carry
 
-    lax.fori_loop(0, width // SUB, to_times, 0)
+    lax.fori_loop(0, LANES // SUB, step, 0)
+
+
+def solve_early_kernel(here_ref, g_ref, diag_ref, lon_ref, lat_ref, c_ref, z0, z1, z2, z3, keep_ref, t_ref, line_ref, tile_ref, p_ref, *work):
+    times, _, rows = t_ref.shape
+    lats = g_ref.shape[0] // times
+    rl = rows // lats
     for t in range(times):
-        for h in range(tiles):
-            turned = t_ref[t, h * LANES : (h + 1) * LANES, :].T
-            for l in range(lats):
-                out_ref[t * lats + l, h * rl : (h + 1) * rl, :] = turned[l * rl : (l + 1) * rl]
+        turned = jnp.concatenate([g_ref[t * lats + l, :rl, :] for l in range(lats)], 0).T
+        t_ref[t, HALO : HALO + LANES, :] = turned
+    per = LANES // (2 * HALO)
+    for g in range(times // per):
+        for l in range(lats):
+            got = halo_group([g_ref[(g * per + n) * lats + l, rl:, :] for n in range(per)], 2 * HALO)
+            for q, piece in enumerate(got):
+                tile_ref[l * rl + q * SUB : l * rl + (q + 1) * SUB, :] = piece
+        turned = tile_ref[...].T
+        for n in range(per):
+            t_ref[g * per + n, :HALO, :] = turned[n * 2 * HALO : n * 2 * HALO + HALO]
+            t_ref[g * per + n, HALO + LANES :, :] = turned[n * 2 * HALO + HALO : (n + 1) * 2 * HALO]
+    to_frequencies(t_ref, line_ref, 0)
+    keep_ref[...] = line_ref[LANES * times :, :]
+    solve_columns(0, (diag_ref, lon_ref, lat_ref), c_ref, p_ref, work, line_ref)
+    to_times(line_ref, t_ref)
+    for q, ref in enumerate((z0, z1, z2, z3)):
+        for p in range(2):
+            tile_ref[...] = t_ref[relative(here_ref[0], 2 * q + p), :LANES, :].T
+            for r in range(lats):
+                lo = pl.multiple_of(relative(here_ref[1], r) * rl, SUB)
+                ref[p, r] = tile_ref[pl.ds(lo, rl), :]
+
+
+def solve_late_kernel(here_ref, z0, z1, z2, z3, keep_ref, diag_ref, lon_ref, lat_ref, c_ref, out_ref, t_ref, line_ref, tile_ref, p_ref, *work):
+    times, _, rows = t_ref.shape
+    lats = out_ref.shape[0] // times
+    rl = rows // lats
+    for q, ref in enumerate((z0, z1, z2, z3)):
+        for p in range(2):
+            for r in range(lats):
+                lo = pl.multiple_of(relative(here_ref[1], r) * rl, SUB)
+                tile_ref[pl.ds(lo, rl), :] = ref[p, r]
+            t_ref[relative(here_ref[0], 2 * q + p), 2 * HALO :, :] = tile_ref[...].T
+    line_ref[: 2 * HALO * times, :] = keep_ref[...]
+    to_frequencies(t_ref, line_ref, 2 * HALO)
+    solve_columns(LANES, (diag_ref, lon_ref, lat_ref), c_ref, p_ref, work, line_ref)
+    to_times(line_ref, t_ref)
+    for t in range(times):
+        turned = t_ref[t, :LANES, :].T
+        for l in range(lats):
+            out_ref[t * lats + l] = turned[l * rl : (l + 1) * rl]
 
 
 def sweep_kernel(width, b_ref, diag_ref, lon_ref, lat_ref, c_ref, p_ref, q_ref):
@@ -344,21 +434,15 @@
 SMEM = pl.BlockSpec(memory_space=pltpu.SMEM)
 
 
+PACK_PARAMS = pltpu.CompilerParams(vmem_limit_bytes=63 << 20)
+
+
 def params(limit=None):
     return pltpu.CompilerParams(vmem_limit_bytes=limit)
 
 
-def gather_rows(block, axis):
-    count = lax.axis_size(axis)
-    me = lax.axis_index(axis)
-    got = block[None]
-    step = 1
-    while step < count:
-        other = lax.ppermute(got, axis, [(i, i ^ step) for i in range(count)])
-        low = (me & step) == 0
-        got = jnp.concatenate([jnp.where(low, got, other), jnp.where(low, other, got)], 0)
-        step *= 2
-    return got
+def called(kernel, **settings):
+    return pl.pallas_call(kernel, **settings)
 
 
 def solve_packed(states, mass_term, lat_coupling, lon_coupling):
@@ -369,75 +453,124 @@
     full = width + 2 * HALO
     height = full * rl // LANES
     f32 = jnp.float32
-    step = PACK_BANDS * width
-    tiles = nlon // LANES
-    send = pl.pallas_call(
-        lambda *refs: pack_kernel(width, *refs),
-        grid=(times // PACK_BANDS,),
-        out_shape=jax.ShapeDtypeStruct((times, lats, height, LANES), f32),
-        in_specs=[
-            pl.BlockSpec((fields, rl, step), lambda i: (0, 0, i)),
-            pl.BlockSpec((fields, rl, LANES), lambda i: (0, 0, (i * (step // LANES) + tiles - 1) % tiles)),
-            pl.BlockSpec((fields, rl, LANES), lambda i: (0, 0, ((i + 1) * (step // LANES)) % tiles)),
+    part = LANES + 2 * HALO
+    fast = params(16 << 20)
+
+    def shaped(*shape):
+        return jax.ShapeDtypeStruct(shape, f32)
+
+    def cost(size, flops=0):
+        return pl.CostEstimate(flops=flops, transcendentals=0, bytes_accessed=8 * size)
+
+    def swap(array, axis, turn):
+        count = lax.axis_size(axis)
+        return lax.ppermute(array, axis, [(n, n ^ turn) for n in range(count)])
+
+    here = jnp.stack([lax.axis_index("tm"), lax.axis_index("lat")]).astype(jnp.int32)
+    local = states.reshape(fields, rl, nlon)
+    edge = part * rl // LANES
+    held = times * rl
+    dma = pltpu.SemaphoreType.DMA
+    HBM = pl.BlockSpec(memory_space=pltpu.MemorySpace.HBM)
+    early, *late = pl.pallas_call(
+        pack_kernel,
+        out_shape=(shaped(times, fields, edge, LANES),) + (shaped(held + 3 * height, LANES),) * lats,
+        in_specs=[SMEM] + [HBM] * 4,
+        out_specs=(HBM,) * (lats + 1),
+        scratch_shapes=[
+            pltpu.VMEM((fields, rl, nlon), f32),
+            pltpu.VMEM((fields, times, edge, LANES), f32),
+            pltpu.VMEM((lats, held, LANES), f32),
+            pltpu.VMEM((3, rl, LANES), f32),
+            pltpu.VMEM((3, rl, width), f32),
+            pltpu.VMEM((3, rl, LANES), f32),
+            pltpu.VMEM((3 * height, LANES), f32),
+            dma((fields,)),
+            dma((9,)),
+            dma((fields,)),
+            dma((2 * lats,)),
         ],
-        out_specs=pl.BlockSpec((PACK_BANDS, lats, height, LANES), lambda i: (i, 0, 0, 0)),
-        cost_estimate=pl.CostEstimate(flops=0, transcendentals=0, bytes_accessed=8 * states.size),
-        compiler_params=params(16 << 20),
+        cost_estimate=cost(states.size),
+        compiler_params=PACK_PARAMS,
         name="pack",
-    )(*[states.reshape(fields, rl, nlon)] * 3)
-    band = lax.axis_index("tm").astype(jnp.int32).reshape(1)
-    coef = pl.pallas_call(
-        lambda *refs: pack_coef_kernel(width, *refs),
-        out_shape=jax.ShapeDtypeStruct((3, height, LANES), f32),
-        in_specs=[SMEM] + [VMEM] * 3,
-        out_specs=VMEM,
-        cost_estimate=pl.CostEstimate(flops=0, transcendentals=0, bytes_accessed=16 * mass_term.size),
-        compiler_params=params(16 << 20),
-        name="pack_coefficients",
-    )(band, mass_term, lat_coupling, lon_coupling)
-    coefs = gather_rows(coef, "lat")
-    got = lax.all_to_all(send.reshape(times * lats, height, LANES), ("tm", "lat"), 0, 0, tiled=True)
-    groups = LANES // times
-    columns = full // groups
-    slab = ((rows + PAD) * columns + PAD, LANES)
-    flat = (rows * columns, LANES)
-    diag, lon, lat = pl.pallas_call(
-        lambda *refs: coef_kernel(width, times, *refs),
-        out_shape=(jax.ShapeDtypeStruct(flat, f32),) * 2 + (jax.ShapeDtypeStruct(slab, f32),),
-        in_specs=[VMEM],
+    )(here, local, mass_term, lat_coupling, lon_coupling)
+    late = [late[0]] + [swap(late[r], "lat", r) for r in range(1, lats)]
+    early = lax.all_to_all(early.reshape(times * lats, edge, LANES), ("tm", "lat"), 0, 0, tiled=True)
+    coefs = pl.pallas_call(
+        lambda *refs: coef_kernel(held, *refs),
+        out_shape=(shaped(full, rows),) * 3,
+        in_specs=[SMEM] + [VMEM] * lats,
         out_specs=(VMEM,) * 3,
         scratch_shapes=[pltpu.VMEM((3, full, rows), f32), pltpu.VMEM((rows, LANES), f32)],
-        cost_estimate=pl.CostEstimate(flops=30 * full * rows, transcendentals=0, bytes_accessed=128 * full * rows),
-        compiler_params=params(16 << 20),
+        cost_estimate=cost(6 * full * rows, 30 * full * rows),
+        compiler_params=fast,
         name="coefficients",
-    )(coefs)
+    )(here, *late)
+
+    zs = times // 2
+    block = (rl, LANES)
+
+    def of(p, q):
+        return slice((p * zs + q) * rl, (p * zs + q + 1) * rl)
+
+    plan = [(0, (r, q), r, of(1, q)) for r in range(lats) for q in range(zs)]
+    other = shuffle(plan, late, [(lats, zs) + block])[0]
+    other = swap(other, "tm", 1)
+    plan = [(q, (0, r), r, of(0, q)) for r in range(lats) for q in range(zs)]
+    plan += [(q, (1, r), lats, (r, q)) for r in range(lats) for q in range(zs)]
+    inward = shuffle(plan, late + [other], [(2, lats) + block] * zs)
+    inward = [inward[0]] + [swap(inward[q], "tm", 2 * q) for q in range(1, zs)]
+
+    groups = LANES // times
+    columns = part // groups
+    slab = pltpu.VMEM(((rows + PAD) * columns + PAD, LANES), f32)
+    flat = pltpu.VMEM((rows * columns, LANES), f32)
+    scratch = [pltpu.VMEM((times, part, rows), f32), pltpu.VMEM((part * times, rows), f32), pltpu.VMEM((rows, LANES), f32)]
+    scratch += [slab, slab, slab, flat, flat, slab]
     basis = time_basis(times)
     scale = np.max(np.abs(basis), 1) ** 2
     scale = np.where(scale > 1.5 / times, 2.0 / times, 1.0 / times)
     c_rows = jnp.asarray(np.tile(weights(times) * scale[None, :], (1, groups)), f32)
-    out = pl.pallas_call(
-        lambda *refs: solve_kernel(width, *refs),
-        out_shape=jax.ShapeDtypeStruct((times * lats, width * rl // LANES, LANES), f32),
-        in_specs=[VMEM] * 5,
+    work = cost(part * times * rows, 16 * SWEEPS * part * times * rows)
+    *outward, keep = called(
+        solve_early_kernel,
+        out_shape=(shaped(2, lats, *block),) * zs + (shaped(2 * HALO * times, rows),),
+        in_specs=[SMEM] + [VMEM] * 5,
+        out_specs=(VMEM,) * (zs + 1),
+        scratch_shapes=scratch,
+        cost_estimate=work,
+        compiler_params=params(24 << 20),
+        name="solve_early",
+    )(here, early, *coefs, c_rows)
+    outward = [outward[0]] + [swap(outward[q], "tm", 2 * q) for q in range(1, zs)]
+    out = called(
+        solve_late_kernel,
+        out_shape=shaped(times * lats, *block),
+        in_specs=[SMEM] + [VMEM] * (zs + 5),
         out_specs=VMEM,
-        scratch_shapes=[pltpu.VMEM(slab, f32)] * 3
-        + [pltpu.VMEM((full * times, rows), f32), pltpu.VMEM((times, full, rows), f32), pltpu.VMEM((rows, LANES), f32)],
-        cost_estimate=pl.CostEstimate(
-            flops=12 * SWEEPS * full * times * rows, transcendentals=0, bytes_accessed=8 * full * times * rows
-        ),
+        scratch_shapes=scratch,
+        cost_estimate=work,
         compiler_params=params(24 << 20),
-        name="solve",
-    )(got, diag, lon, lat, c_rows)
+        name="solve_late",
+    )(here, *inward, keep, *coefs, c_rows)
     back = lax.all_to_all(out, ("tm", "lat"), 0, 0, tiled=True)
+
+    plan = [(0, (q, r), q, (1, r)) for r in range(lats) for q in range(zs)]
+    other = shuffle(plan, outward, [(zs, lats) + block])[0]
+    other = swap(other, "tm", 1)
+    plan = [(r, q, q, (0, r)) for r in range(lats) for q in range(zs)]
+    plan += [(r, zs + q, zs, (q, r)) for r in range(lats) for q in range(zs)]
+    home = shuffle(plan, outward + [other], [(times,) + block] * lats)
+    home = [home[0]] + [swap(home[r], "lat", r) for r in range(1, lats)]
     result = pl.pallas_call(
-        lambda *refs: unpack_kernel(width, *refs),
-        out_shape=jax.ShapeDtypeStruct((fields, rl, nlon), f32),
-        in_specs=[VMEM],
+        unpack_kernel,
+        out_shape=shaped(fields, rl, nlon),
+        in_specs=[SMEM] + [VMEM] * (lats + 1),
         out_specs=VMEM,
-        cost_estimate=pl.CostEstimate(flops=0, transcendentals=0, bytes_accessed=8 * states.size),
-        compiler_params=params(16 << 20),
+        cost_estimate=cost(states.size),
+        compiler_params=fast,
         name="unpack",
-    )(back)
+    )(here, back, *home)
     return result.reshape(states.shape)
 
 
@@ -495,9 +628,8 @@
 def per_device(states, mass_term, lat_coupling, lon_coupling):
     fields, tl, rl, nlon = states.shape
     tm, lats = lax.axis_size("tm"), lax.axis_size("lat")
-    packed = tl == 1 and tm == SUB and lats == fields and rl * lats == LANES
-    packed = packed and nlon % (tm * LANES) == 0 and 2 * HALO * rl == SUB * LANES
-    packed = packed and (nlon // tm + 2 * HALO) % (LANES // tm) == 0 and tm % PACK_BANDS == 0
+    packed = tl == 1 and tm == SUB and lats == fields == 4 and rl * lats == LANES
+    packed = packed and nlon == 2 * tm * LANES and 2 * HALO * rl == SUB * LANES
     plan = solve_packed if packed else solve_general
     return plan(states, mass_term, lat_coupling, lon_coupling)
 

time: 85 us -> 97.8 us (1.15)
  blocking collectives: 29.9 us -> 0 us
  waiting for transfers between devices: 23 us -> 47.5 us
  starting transfers between devices: 9.67 us -> 26.9 us
  Pallas kernels: 16.2 us -> 22.4 us
  local copies, waits for them, and re-layouts: 5.82 us -> 0.02 us
    all_to_all x1 -> x0, blocking collectives: 29.9 us -> none  [solve_packed(): back = lax.all_to_all(out, ('tm', 'lat'), 0, 0, tiled=True)]
    ppermute x2 -> x14, waiting for transfers between devices: 20 us -> 47.5 us  [swap(): return lax.ppermute(array, axis, [(n, n ^ turn) for n in range(count)])]
    ppermute x2 -> x14, starting transfers between devices: 2.35 us -> 16.2 us  [swap(): return lax.ppermute(array, axis, [(n, n ^ turn) for n in range(count)])]
    pallas_call x5 -> x9, Pallas kernels: 16.2 us -> 22.4 us  [the longest x1 8.33 us: solve_packed(): called(solve_late_kernel, out_shape=shaped(times * lats, *block), in_spec...]
    unnamed x18 -> x12, local copies, waits for them, and re-layouts: 5.82 us -> 0.02 us
    all_to_all x1 -> x2, starting transfers between devices: 7.33 us -> 10.7 us  [the longest x1 7.33 us: solve_packed(): lax.all_to_all(early.reshape(times * lats, edge, LANES), ('tm', 'lat'), 0...]
    all_to_all x1 -> x2, waiting for transfers between devices: 3.01 us -> 0.01 us  [the longest x1 0.01 us: solve_packed(): lax.all_to_all(early.reshape(times * lats, edge, LANES), ('tm', 'lat'), 0...]
  transfers between devices with their start and end apart: 3 -> 16, of which waited for: 3 -> 9; matrix products, arithmetic and copies ran while one was open for 0% -> 0% of each run, Pallas kernels for 2% -> 9%
where the time goes in v2:
time: 97.8 us; the launch traced here: 97.6 us
  waiting for transfers between devices  47.5 us (49%)
  starting transfers between devices  26.9 us (28%)
  Pallas kernels  22.4 us (23%)
    ppermute x14, waiting for transfers between devices, swap(): return lax.ppermute(array, axis, [(n, n ^ turn) for n in range(count)])  47.5 us
    ppermute x14, starting transfers between devices, swap(): return lax.ppermute(array, axis, [(n, n ^ turn) for n in range(count)])  16.2 us
    pallas_call x1, Pallas kernels, solve_packed(): called(solve_late_kernel, out_shape=shaped(times * lats, *block), in_spec...  8.33 us
    pallas_call x1, Pallas kernels, solve_packed(): called(solve_early_kernel, out_shape=(shaped(2, lats, *block),) * zs + (s...  7.8 us
    all_to_all x1, starting transfers between devices, solve_packed(): lax.all_to_all(early.reshape(times * lats, edge, LANES), ('tm', 'lat'), 0...  7.33 us
    pallas_call x1, Pallas kernels, solve_packed(): pl.pallas_call(pack_kernel, out_shape=(shaped(times, fields, edge, LANES)...  3.61 us
    all_to_all x1, starting transfers between devices, solve_packed(): back = lax.all_to_all(out, ('tm', 'lat'), 0, 0, tiled=True)  3.37 us
  transfers between devices with their start and end apart: 16, of which 9 were waited for; matrix products, arithmetic and copies ran while one was open for 0% of the time, Pallas kernels for 9%

profile of v2, /device:TPU:0, one launch (start us, length us, event | category | flops | bytes accessed | tf_op | source)
XLA Modules:
  0.0 97.6 jit_solution(703742061253284302)
XLA Ops:
  0.0 0.7 pad_add_fusion.here_ref.refs_0_
  0.7 3.6 %pack.1 = (f32[8,4,40,128]{3,2,1,0:T(8,128)}, f32[472,128]{1,0:T(8,128)}, f32[472,128]{1,0:T(8,128)}, f32[472,128]{1,0:T(8,128)}, f32[472,128]{1,0:T(8,128)}) custom-call(s32[2]{0:T(128)} %pad_add_fusion.here_ref.refs_0_, f32[4,32,2048]{2,1,0:T(8,128)} %bitcast.7, f32[32,2048]{1,0:T(8,128)} %refs_0_.1, f32[32,2048]{1,0:T(8,128)} %refs_1_.1, f32[32,2048]{1,0:T(8,128)} %refs_2_.1), custom_call_target="tpu_custom_call" | custom-call | bytes 2097152 | tf_op jit(solution)/shard_map/pack/pallas_call | solution.py:475
  4.3 0.0 copy-start.5
  4.3 0.0 copy-start.4
  4.3 0.0 copy-start.3
  4.3 0.0 copy-start
  4.3 7.3 %all-to-all-start = ((f32[32,40,128]{2,1,0:T(8,128)}), f32[32,40,128]{2,1,0:T(8,128)S(1)}, u32[]{:S(2)}, u32[]{:S(2)}) async-start(f32[32,40,128]{2,1,0:T(8,128)} %bitcast.8), calls=%async_computation | async-start | bytes 1310720 | tf_op jit(solution)/shard_map/all_to_all | solution.py:498
  11.6 0.0 copy-done.5
  11.7 1.8 %collective-permute-start = (f32[472,128]{1,0:T(8,128)S(1)}, f32[472,128]{1,0:T(8,128)S(1)}, u32[]{:S(2)}, u32[]{:S(2)}) collective-permute-start(f32[472,128]{1,0:T(8,128)S(1)} %copy-done.5), channel_id=1, source_target_pairs={{0,1},{1,0},{2,3},{3,2},{4,5},{5,4},{6,7},{7,6},{8,9},{9,8},{10,11... | collective-permute-start | bytes 725000 | tf_op jit(solution)/shard_map/ppermute | solution.py:467
  13.5 0.0 copy-done.4
  13.5 1.5 %collective-permute-start.1 = (f32[472,128]{1,0:T(8,128)S(1)}, f32[472,128]{1,0:T(8,128)S(1)}, u32[]{:S(2)}, u32[]{:S(2)}) collective-permute-start(f32[472,128]{1,0:T(8,128)S(1)} %copy-done.4), channel_id=1, source_target_pairs={{0,2},{1,3},{2,0},{3,1},{4,6},{5,7},{6,4},{7,5},{8,10},{9,11},{10,... | collective-permute-start | bytes 725000 | tf_op jit(solution)/shard_map/ppermute | solution.py:467
  15.0 0.0 copy-done.3
  15.0 0.3 collective-permute-start.2
  15.2 10.9 %collective-permute-done.refs_1_.refs_2_ = f32[472,128]{1,0:T(8,128)S(1)} collective-permute-done((f32[472,128]{1,0:T(8,128)S(1)}, f32[472,128]{1,0:T(8,128)S(1)}, u32[]{:S(2)}, u32[]{:S(2)}) %collective-permute-start) | collective-permute-done | bytes 241696 | tf_op jit(solution)/shard_map/ppermute | solution.py:467
  26.2 0.0 collective-permute-done.1.refs_2_.refs_3_
  26.2 6.8 %collective-permute-done.2.refs_3_.refs_4_ = f32[472,128]{1,0:T(8,128)S(1)} collective-permute-done((f32[472,128]{1,0:T(8,128)S(1)}, f32[472,128]{1,0:T(8,128)S(1)}, u32[]{:S(2)}, u32[]{:S(2)}) %collective-permute-start.2) | collective-permute-done | bytes 241696 | tf_op jit(solution)/shard_map/ppermute | solution.py:467
  33.0 0.0 copy-done
  33.0 0.1 collective-permute-start.3
  33.1 1.5 %collective-permute-done.3.refs_4_ = f32[4,4,32,128]{3,2,1,0:T(8,128)S(1)} collective-permute-done((f32[4,4,32,128]{3,2,1,0:T(8,128)S(1)}, f32[4,4,32,128]{3,2,1,0:T(8,128)S(1)}, u32[]{:S(2)}, u32[]{:S(2)}) %collective-permute-start.3) | collective-permute-done | bytes 262176 | tf_op jit(solution)/shard_map/ppermute | solution.py:467
  34.6 1.5 %collective-permute-start.4 = (f32[2,4,32,128]{3,2,1,0:T(8,128)S(1)}, f32[2,4,32,128]{3,2,1,0:T(8,128)S(1)}, u32[]{:S(2)}, u32[]{:S(2)}) collective-permute-start(f32[2,4,32,128]{3,2,1,0:T(8,128)S(1)} %get-tuple-element.31), channel_id=1, source_target_pairs={{0,8},{4,12},{8,0},{12,4},{16,24},{20,28},{24,16},{28,20},{1,9},{5... | collective-permute-start | bytes 393224 | tf_op jit(solution)/shard_map/ppermute | solution.py:467
  36.2 2.3 %collective-permute-start.5 = (f32[2,4,32,128]{3,2,1,0:T(8,128)S(1)}, f32[2,4,32,128]{3,2,1,0:T(8,128)S(1)}, u32[]{:S(2)}, u32[]{:S(2)}) collective-permute-start(f32[2,4,32,128]{3,2,1,0:T(8,128)S(1)} %get-tuple-element.32), channel_id=1, source_target_pairs={{0,16},{4,20},{8,24},{12,28},{16,0},{20,4},{24,8},{28,12},{1,17},{... | collective-permute-start | bytes 393224 | tf_op jit(solution)/shard_map/ppermute | solution.py:467
  38.4 0.7 collective-permute-start.6
  39.1 0.0 copy-done.2
  39.1 1.0 %coefficients.1 = (f32[288,128]{1,0:T(8,128)S(1)}, f32[288,128]{1,0:T(8,128)S(1)}, f32[288,128]{1,0:T(8,128)S(1)}) custom-call(s32[2]{0:T(128)S(1)} %copy-done.2, f32[472,128]{1,0:T(8,128)S(1)} %copy-done, f32[472,128]{1,0:T(8,128)S(1)} %collective-permute-done.refs_1_.refs_2_, f32[472,128]{1,0:T(8,128)S(1)} %collective-permute-done.1.refs_2_.refs_3_, ...), custom_call_target="tpu_custom_call" | custom-call | flops 1105920 | bytes 1769472 | tf_op jit(solution)/shard_map/coefficients/pallas_call | solution.py:499
  40.1 0.0 all-to-all-done.g_ref
  40.1 0.0 copy-done.1
  40.1 7.8 %solve_early.1 = (f32[2,4,32,128]{3,2,1,0:T(8,128)S(1)}, f32[2,4,32,128]{3,2,1,0:T(8,128)S(1)}, f32[2,4,32,128]{3,2,1,0:T(8,128)S(1)}, f32[2,4,32,128]{3,2,1,0:T(8,128)S(1)}, f32[256,128]{1,0:T(8,128)S(1)}) custom-call(s32[2]{0:T(128)S(1)} %copy-done.2, f32[32,40,128]{2,1,0:T(8,128)S(1)} %all-to-all-done.g_ref, f32[288,128]{1,0:T(8,128)S(1)} %get-tuple-element.35.diag_ref, ...), custom_call_target="tpu_custom_call" | custom-call | flops 41943040 | bytes 1310720 | tf_op jit(solution)/shard_map/solve_early/pallas_call | solution.py:535
  47.9 0.0 collective-permute-done.4.z1
  47.9 1.1 %collective-permute-done.5.z2 = f32[2,4,32,128]{3,2,1,0:T(8,128)S(1)} collective-permute-done((f32[2,4,32,128]{3,2,1,0:T(8,128)S(1)}, f32[2,4,32,128]{3,2,1,0:T(8,128)S(1)}, u32[]{:S(2)}, u32[]{:S(2)}) %collective-permute-start.5) | collective-permute-done | bytes 131104 | tf_op jit(solution)/shard_map/ppermute | solution.py:467
  49.0 0.0 collective-permute-done.6.z3
  49.0 8.3 %solve_late.1 = f32[32,32,128]{2,1,0:T(8,128)} custom-call(s32[2]{0:T(128)S(1)} %copy-done.2, f32[2,4,32,128]{3,2,1,0:T(8,128)S(1)} %get-tuple-element.30.z0, f32[2,4,32,128]{3,2,1,0:T(8,128)S(1)} %collective-permute-done.4.z1, f32[2,4,32,128]{3,2,1,0:T(8,128)S(1)} %collective-permute-done.5.z2, f32[2,4,32,128]{3,2,1,0:T(8,128)S(1)} %collective-permute-done.6.z3, ...), custom_call_target="tpu_custom_call" | custom-call | flops 41943040 | bytes 1310720 | tf_op jit(solution)/shard_map/solve_late/pallas_call | solution.py:546
  57.4 3.4 %all-to-all-start.1 = ((f32[32,32,128]{2,1,0:T(8,128)}), f32[32,32,128]{2,1,0:T(8,128)S(1)}, u32[]{:S(2)}, u32[]{:S(2)}) async-start(f32[32,32,128]{2,1,0:T(8,128)} %solve_late.1), calls=%async_computation.1 | async-start | bytes 1048576 | tf_op jit(solution)/shard_map/all_to_all | solution.py:556
  60.7 1.8 %collective-permute-start.7 = (f32[2,4,32,128]{3,2,1,0:T(8,128)S(1)}, f32[2,4,32,128]{3,2,1,0:T(8,128)S(1)}, u32[]{:S(2)}, u32[]{:S(2)}) collective-permute-start(f32[2,4,32,128]{3,2,1,0:T(8,128)S(1)} %get-tuple-element.40), channel_id=1, source_target_pairs={{0,8},{4,12},{8,0},{12,4},{16,24},{20,28},{24,16},{28,20},{1,9},{5... | collective-permute-start | bytes 393224 | tf_op jit(solution)/shard_map/ppermute | solution.py:467
  62.6 2.4 %collective-permute-start.8 = (f32[2,4,32,128]{3,2,1,0:T(8,128)S(1)}, f32[2,4,32,128]{3,2,1,0:T(8,128)S(1)}, u32[]{:S(2)}, u32[]{:S(2)}) collective-permute-start(f32[2,4,32,128]{3,2,1,0:T(8,128)S(1)} %get-tuple-element.41), channel_id=1, source_target_pairs={{0,16},{4,20},{8,24},{12,28},{16,0},{20,4},{24,8},{28,12},{1,17},{... | collective-permute-start | bytes 393224 | tf_op jit(solution)/shard_map/ppermute | solution.py:467
  65.0 0.2 collective-permute-start.9
  65.2 8.7 %collective-permute-done.7.refs_1_ = f32[2,4,32,128]{3,2,1,0:T(8,128)S(1)} collective-permute-done((f32[2,4,32,128]{3,2,1,0:T(8,128)S(1)}, f32[2,4,32,128]{3,2,1,0:T(8,128)S(1)}, u32[]{:S(2)}, u32[]{:S(2)}) %collective-permute-start.7) | collective-permute-done | bytes 131104 | tf_op jit(solution)/shard_map/ppermute | solution.py:467
  73.9 10.8 %collective-permute-done.8.refs_2_ = f32[2,4,32,128]{3,2,1,0:T(8,128)S(1)} collective-permute-done((f32[2,4,32,128]{3,2,1,0:T(8,128)S(1)}, f32[2,4,32,128]{3,2,1,0:T(8,128)S(1)}, u32[]{:S(2)}, u32[]{:S(2)}) %collective-permute-start.8) | collective-permute-done | bytes 131104 | tf_op jit(solution)/shard_map/ppermute | solution.py:467
  84.7 0.0 collective-permute-done.9.refs_3_
  84.7 0.1 collective-permute-start.10
  84.8 1.5 %collective-permute-done.10.refs_4_ = f32[4,4,32,128]{3,2,1,0:T(8,128)S(1)} collective-permute-done((f32[4,4,32,128]{3,2,1,0:T(8,128)S(1)}, f32[4,4,32,128]{3,2,1,0:T(8,128)S(1)}, u32[]{:S(2)}, u32[]{:S(2)}) %collective-permute-start.10) | collective-permute-done | bytes 262176 | tf_op jit(solution)/shard_map/ppermute | solution.py:467
  86.4 1.5 %collective-permute-start.11 = (f32[8,32,128]{2,1,0:T(8,128)S(1)}, f32[8,32,128]{2,1,0:T(8,128)S(1)}, u32[]{:S(2)}, u32[]{:S(2)}) collective-permute-start(f32[8,32,128]{2,1,0:T(8,128)S(1)} %get-tuple-element.44), channel_id=1, source_target_pairs={{0,1},{1,0},{2,3},{3,2},{4,5},{5,4},{6,7},{7,6},{8,9},{9,8},{10,11... | collective-permute-start | bytes 393224 | tf_op jit(solution)/shard_map/ppermute | solution.py:467
  87.9 1.5 %collective-permute-start.12 = (f32[8,32,128]{2,1,0:T(8,128)S(1)}, f32[8,32,128]{2,1,0:T(8,128)S(1)}, u32[]{:S(2)}, u32[]{:S(2)}) collective-permute-start(f32[8,32,128]{2,1,0:T(8,128)S(1)} %get-tuple-element.45), channel_id=1, source_target_pairs={{0,2},{1,3},{2,0},{3,1},{4,6},{5,7},{6,4},{7,5},{8,10},{9,11},{10,... | collective-permute-start | bytes 393224 | tf_op jit(solution)/shard_map/ppermute | solution.py:467
  89.4 0.5 collective-permute-start.13
  89.9 2.5 %collective-permute-done.11.refs_1_ = f32[8,32,128]{2,1,0:T(8,128)S(1)} collective-permute-done((f32[8,32,128]{2,1,0:T(8,128)S(1)}, f32[8,32,128]{2,1,0:T(8,128)S(1)}, u32[]{:S(2)}, u32[]{:S(2)}) %collective-permute-start.11) | collective-permute-done | bytes 131104 | tf_op jit(solution)/shard_map/ppermute | solution.py:467
  92.4 3.6 %collective-permute-done.12.refs_2_ = f32[8,32,128]{2,1,0:T(8,128)S(1)} collective-permute-done((f32[8,32,128]{2,1,0:T(8,128)S(1)}, f32[8,32,128]{2,1,0:T(8,128)S(1)}, u32[]{:S(2)}, u32[]{:S(2)}) %collective-permute-start.12) | collective-permute-done | bytes 131104 | tf_op jit(solution)/shard_map/ppermute | solution.py:467
  96.0 0.0 collective-permute-done.13.refs_3_
  96.0 0.0 all-to-all-done.1.g_ref
  96.0 1.6 %unpack.1 = f32[4,32,2048]{2,1,0:T(8,128)} custom-call(s32[2]{0:T(128)S(1)} %copy-done.2, f32[32,32,128]{2,1,0:T(8,128)S(1)} %all-to-all-done.1.g_ref, f32[8,32,128]{2,1,0:T(8,128)S(1)} %get-tuple-element.43.refs_0_, f32[8,32,128]{2,1,0:T(8,128)S(1)} %collective-permute-done.11.refs_1_, f32[8,32,128]{2,1,0:T(8,128)S(1)} %collective-permute-done.12.refs_2_, ...), custom_call_target="tpu_custom_call" | custom-call | bytes 2097152 | tf_op jit(solution)/shard_map/unpack/pallas_call | solution.py:565
  (6 shorter events, 0.1 us)
Async XLA Ops:
  4.3 7.4 %copy-start.5 = (f32[472,128]{1,0:T(8,128)S(1)}, f32[472,128]{1,0:T(8,128)}, u32[]{:S(2)}) copy-start(f32[472,128]{1,0:T(8,128)} %get-tuple-element.27) | copy-start | bytes 724996
  4.3 9.2 %copy-start.4 = (f32[472,128]{1,0:T(8,128)S(1)}, f32[472,128]{1,0:T(8,128)}, u32[]{:S(2)}) copy-start(f32[472,128]{1,0:T(8,128)} %get-tuple-element.28) | copy-start | bytes 724996
  4.3 10.7 %copy-start.3 = (f32[472,128]{1,0:T(8,128)S(1)}, f32[472,128]{1,0:T(8,128)}, u32[]{:S(2)}) copy-start(f32[472,128]{1,0:T(8,128)} %get-tuple-element.29) | copy-start | bytes 724996
  4.3 28.7 %copy-start = (f32[472,128]{1,0:T(8,128)S(1)}, f32[472,128]{1,0:T(8,128)}, u32[]{:S(2)}) copy-start(f32[472,128]{1,0:T(8,128)} %get-tuple-element.26.refs_0_.refs_1_) | copy-start | bytes 724996
  4.3 35.8 %all-to-all-start = ((f32[32,40,128]{2,1,0:T(8,128)}), f32[32,40,128]{2,1,0:T(8,128)S(1)}, u32[]{:S(2)}, u32[]{:S(2)}) async-start(f32[32,40,128]{2,1,0:T(8,128)} %bitcast.8), calls=%async_computation | async-start | bytes 1310720 | tf_op jit(solution)/shard_map/all_to_all | solution.py:498
  11.7 14.5 %collective-permute-start = (f32[472,128]{1,0:T(8,128)S(1)}, f32[472,128]{1,0:T(8,128)S(1)}, u32[]{:S(2)}, u32[]{:S(2)}) collective-permute-start(f32[472,128]{1,0:T(8,128)S(1)} %copy-done.5), channel_id=1, source_target_pairs={{0,1},{1,0},{2,3},{3,2},{4,5},{5,4},{6,7},{7,6},{8,9},{9,8},{10,11... | collective-permute-start | bytes 725000 | tf_op jit(solution)/shard_map/ppermute | solution.py:467
  13.5 12.7 %collective-permute-start.1 = (f32[472,128]{1,0:T(8,128)S(1)}, f32[472,128]{1,0:T(8,128)S(1)}, u32[]{:S(2)}, u32[]{:S(2)}) collective-permute-start(f32[472,128]{1,0:T(8,128)S(1)} %copy-done.4), channel_id=1, source_target_pairs={{0,2},{1,3},{2,0},{3,1},{4,6},{5,7},{6,4},{7,5},{8,10},{9,11},{10,... | collective-permute-start | bytes 725000 | tf_op jit(solution)/shard_map/ppermute | solution.py:467
  15.0 18.0 %collective-permute-start.2 = (f32[472,128]{1,0:T(8,128)S(1)}, f32[472,128]{1,0:T(8,128)S(1)}, u32[]{:S(2)}, u32[]{:S(2)}) collective-permute-start(f32[472,128]{1,0:T(8,128)S(1)} %copy-done.3), channel_id=1, source_target_pairs={{0,3},{1,2},{2,1},{3,0},{4,7},{5,6},{6,5},{7,4},{8,11},{9,10},{10,... | collective-permute-start | bytes 725000 | tf_op jit(solution)/shard_map/ppermute | solution.py:467
  33.0 1.6 %collective-permute-start.3 = (f32[4,4,32,128]{3,2,1,0:T(8,128)S(1)}, f32[4,4,32,128]{3,2,1,0:T(8,128)S(1)}, u32[]{:S(2)}, u32[]{:S(2)}) collective-permute-start(f32[4,4,32,128]{3,2,1,0:T(8,128)S(1)} %shard_map.55), channel_id=1, source_target_pairs={{0,4},{4,0},{8,12},{12,8},{16,20},{20,16},{24,28},{28,24},{1,5},{5... | collective-permute-start | bytes 786440 | tf_op jit(solution)/shard_map/ppermute | solution.py:467
  34.6 13.3 %collective-permute-start.4 = (f32[2,4,32,128]{3,2,1,0:T(8,128)S(1)}, f32[2,4,32,128]{3,2,1,0:T(8,128)S(1)}, u32[]{:S(2)}, u32[]{:S(2)}) collective-permute-start(f32[2,4,32,128]{3,2,1,0:T(8,128)S(1)} %get-tuple-element.31), channel_id=1, source_target_pairs={{0,8},{4,12},{8,0},{12,4},{16,24},{20,28},{24,16},{28,20},{1,9},{5... | collective-permute-start | bytes 393224 | tf_op jit(solution)/shard_map/ppermute | solution.py:467
  36.2 2.9 %copy-start.2 = (s32[2]{0:T(128)S(1)}, s32[2]{0:T(128)}, u32[]{:S(2)}) copy-start(s32[2]{0:T(128)} %pad_add_fusion.here_ref.refs_0_) | copy-start | bytes 28
  36.2 12.9 %collective-permute-start.5 = (f32[2,4,32,128]{3,2,1,0:T(8,128)S(1)}, f32[2,4,32,128]{3,2,1,0:T(8,128)S(1)}, u32[]{:S(2)}, u32[]{:S(2)}) collective-permute-start(f32[2,4,32,128]{3,2,1,0:T(8,128)S(1)} %get-tuple-element.32), channel_id=1, source_target_pairs={{0,16},{4,20},{8,24},{12,28},{16,0},{20,4},{24,8},{28,12},{1,17},{... | collective-permute-start | bytes 393224 | tf_op jit(solution)/shard_map/ppermute | solution.py:467
  38.4 10.6 %collective-permute-start.6 = (f32[2,4,32,128]{3,2,1,0:T(8,128)S(1)}, f32[2,4,32,128]{3,2,1,0:T(8,128)S(1)}, u32[]{:S(2)}, u32[]{:S(2)}) collective-permute-start(f32[2,4,32,128]{3,2,1,0:T(8,128)S(1)} %get-tuple-element.33), channel_id=1, source_target_pairs={{0,24},{4,28},{8,16},{12,20},{16,8},{20,12},{24,0},{28,4},{1,25},{... | collective-permute-start | bytes 393224 | tf_op jit(solution)/shard_map/ppermute | solution.py:467
  39.1 1.0 %copy-start.1 = (f32[17,128]{1,0:T(8,128)S(1)}, f32[17,128]{1,0:T(8,128)}, u32[]{:S(2)}) copy-start(f32[17,128]{1,0:T(8,128)} %constant.11.clone.c_ref) | copy-start | bytes 26116
  57.4 38.6 %all-to-all-start.1 = ((f32[32,32,128]{2,1,0:T(8,128)}), f32[32,32,128]{2,1,0:T(8,128)S(1)}, u32[]{:S(2)}, u32[]{:S(2)}) async-start(f32[32,32,128]{2,1,0:T(8,128)} %solve_late.1), calls=%async_computation.1 | async-start | bytes 1048576 | tf_op jit(solution)/shard_map/all_to_all | solution.py:556
  60.7 13.2 %collective-permute-start.7 = (f32[2,4,32,128]{3,2,1,0:T(8,128)S(1)}, f32[2,4,32,128]{3,2,1,0:T(8,128)S(1)}, u32[]{:S(2)}, u32[]{:S(2)}) collective-permute-start(f32[2,4,32,128]{3,2,1,0:T(8,128)S(1)} %get-tuple-element.40), channel_id=1, source_target_pairs={{0,8},{4,12},{8,0},{12,4},{16,24},{20,28},{24,16},{28,20},{1,9},{5... | collective-permute-start | bytes 393224 | tf_op jit(solution)/shard_map/ppermute | solution.py:467
  62.6 22.1 %collective-permute-start.8 = (f32[2,4,32,128]{3,2,1,0:T(8,128)S(1)}, f32[2,4,32,128]{3,2,1,0:T(8,128)S(1)}, u32[]{:S(2)}, u32[]{:S(2)}) collective-permute-start(f32[2,4,32,128]{3,2,1,0:T(8,128)S(1)} %get-tuple-element.41), channel_id=1, source_target_pairs={{0,16},{4,20},{8,24},{12,28},{16,0},{20,4},{24,8},{28,12},{1,17},{... | collective-permute-start | bytes 393224 | tf_op jit(solution)/shard_map/ppermute | solution.py:467
  65.0 19.7 %collective-permute-start.9 = (f32[2,4,32,128]{3,2,1,0:T(8,128)S(1)}, f32[2,4,32,128]{3,2,1,0:T(8,128)S(1)}, u32[]{:S(2)}, u32[]{:S(2)}) collective-permute-start(f32[2,4,32,128]{3,2,1,0:T(8,128)S(1)} %get-tuple-element.42), channel_id=1, source_target_pairs={{0,24},{4,28},{8,16},{12,20},{16,8},{20,12},{24,0},{28,4},{1,25},{... | collective-permute-start | bytes 393224 | tf_op jit(solution)/shard_map/ppermute | solution.py:467
  84.7 1.6 %collective-permute-start.10 = (f32[4,4,32,128]{3,2,1,0:T(8,128)S(1)}, f32[4,4,32,128]{3,2,1,0:T(8,128)S(1)}, u32[]{:S(2)}, u32[]{:S(2)}) collective-permute-start(f32[4,4,32,128]{3,2,1,0:T(8,128)S(1)} %shard_map.57), channel_id=1, source_target_pairs={{0,4},{4,0},{8,12},{12,8},{16,20},{20,16},{24,28},{28,24},{1,5},{5... | collective-permute-start | bytes 786440 | tf_op jit(solution)/shard_map/ppermute | solution.py:467
  86.4 6.0 %collective-permute-start.11 = (f32[8,32,128]{2,1,0:T(8,128)S(1)}, f32[8,32,128]{2,1,0:T(8,128)S(1)}, u32[]{:S(2)}, u32[]{:S(2)}) collective-permute-start(f32[8,32,128]{2,1,0:T(8,128)S(1)} %get-tuple-element.44), channel_id=1, source_target_pairs={{0,1},{1,0},{2,3},{3,2},{4,5},{5,4},{6,7},{7,6},{8,9},{9,8},{10,11... | collective-permute-start | bytes 393224 | tf_op jit(solution)/shard_map/ppermute | solution.py:467
  87.9 8.1 %collective-permute-start.12 = (f32[8,32,128]{2,1,0:T(8,128)S(1)}, f32[8,32,128]{2,1,0:T(8,128)S(1)}, u32[]{:S(2)}, u32[]{:S(2)}) collective-permute-start(f32[8,32,128]{2,1,0:T(8,128)S(1)} %get-tuple-element.45), channel_id=1, source_target_pairs={{0,2},{1,3},{2,0},{3,1},{4,6},{5,7},{6,4},{7,5},{8,10},{9,11},{10,... | collective-permute-start | bytes 393224 | tf_op jit(solution)/shard_map/ppermute | solution.py:467
  89.4 6.6 %collective-permute-start.13 = (f32[8,32,128]{2,1,0:T(8,128)S(1)}, f32[8,32,128]{2,1,0:T(8,128)S(1)}, u32[]{:S(2)}, u32[]{:S(2)}) collective-permute-start(f32[8,32,128]{2,1,0:T(8,128)S(1)} %get-tuple-element.46), channel_id=1, source_target_pairs={{0,3},{1,2},{2,1},{3,0},{4,7},{5,6},{6,5},{7,4},{8,11},{9,10},{10,... | collective-permute-start | bytes 393224 | tf_op jit(solution)/shard_map/ppermute | solution.py:467
